TPU v7x, 128 devices: a whole 4x4x4 slice. The times are simulated.
128 devices in a mesh: row: 8 (over y_lo, z), col: 16 (over x, y_hi, core).
Axes of the slice: x: 4, y: 4 (y_hi: 2, y_lo: 2; y = y_hi * 2 + y_lo), z: 4, core: 2. Of those that a mesh axis runs over, the one named last changes fastest.
Arguments:
- series: bfloat16 [384, 57344], P(None, 'col'), may hold values from -6 to 6
- omega_tiles: float32 [8, 16, 10, 512, 512], P('row', 'col'), may hold values from -3 to 40, as said below
- tile_row: int32 [8, 16, 10], P('row', 'col'), may hold values from 0 to 13, as said below
- tile_col: int32 [8, 16, 10], P('row', 'col'), may hold values from 0 to 6, as said below
- tile_count: int32 [8, 16], P('row', 'col'), may hold values from 1 to 10, as said below
Outputs:
- omega_next: float32 [8, 16, 10, 512, 512], P('row', 'col')
- step_values: float32 [2], replicated
Inputs may be any that keep to these rules, and one draw needn't show every extreme that they name: `tile_row`: the live slots of one device name distinct blocks of its band; every block of the band that lies on the matrix's diagonal is among them; slots that are not live hold 0. `tile_col`: as for tile_row. `tile_count`: some device uses all 10 slots in every draw. `omega_tiles`: diagonal entries of the matrix are positive; slots that are not live are zero.
All inputs are finite; a program needn't handle non-finite values.
Results may differ from a plain program's by a relative error of at most 0.0016.
Values may be sent and summed in bfloat16 or wider, within the bound.
A program may use at most 384 MiB of HBM per device.

v0:
```python
import jax
import jax.numpy as jnp
from jax import lax
from jax.sharding import PartitionSpec as P

step_size = 0.1
penalty = 0.3


def spread(value, axis, source):
    kept = jnp.where(lax.axis_index(axis) == source, value, 0).astype(value.dtype)
    return lax.psum(kept, axis)


def local(series, omega_tiles, tile_row, tile_col, tile_count):
    samples = series.shape[0]
    panel_width = series.shape[1]
    tile_edge = omega_tiles.shape[3]
    slot_total = omega_tiles.shape[2]
    blocks = panel_width // tile_edge
    per_band = lax.axis_size("col") // lax.axis_size("row")
    band_blocks = blocks * per_band
    row_index = lax.axis_index("row")
    col_index = lax.axis_index("col")
    local_rows = tile_row[0, 0]
    local_cols = tile_col[0, 0]
    is_live = (jnp.arange(slot_total, dtype=jnp.int32) < tile_count[0, 0]).astype(jnp.float32)
    tiles_now = omega_tiles[0, 0] * is_live[:, None, None]
    tiles_half = tiles_now.astype(jnp.bfloat16)
    pieces = []
    for offset in range(per_band):
        pieces.append(spread(series, "col", row_index * per_band + offset))
    band_panels = jnp.concatenate(pieces, axis=1)
    own_panels = series.reshape(samples, blocks, tile_edge)
    band_split = band_panels.reshape(samples, band_blocks, tile_edge)
    right_cols = jnp.take(own_panels, local_cols, axis=1)
    left_rows = jnp.take(band_split, local_rows, axis=1)
    pick_rows = (local_rows[:, None] == jnp.arange(band_blocks, dtype=jnp.int32)[None, :]).astype(
        jnp.float32
    ) * is_live[:, None]
    pick_cols = (local_cols[:, None] == jnp.arange(blocks, dtype=jnp.int32)[None, :]).astype(
        jnp.float32
    ) * is_live[:, None]
    row_terms = jnp.einsum(
        "sab,nsb->san", tiles_half, right_cols, preferred_element_type=jnp.float32
    )
    row_partial = jnp.einsum("sr,san->ran", pick_rows, row_terms, precision=lax.Precision.HIGHEST)
    col_terms = jnp.einsum(
        "nsa,sab->snb", left_rows, tiles_half, preferred_element_type=jnp.float32
    )
    col_partial = jnp.einsum("sb,snt->bnt", pick_cols, col_terms, precision=lax.Precision.HIGHEST)
    share_len = samples // lax.axis_size("col")
    row_full = lax.psum(row_partial, "col")
    col_full = lax.psum(col_partial, "row")
    row_piece = lax.dynamic_slice_in_dim(row_full, col_index * share_len, share_len, 2)
    squares = jnp.sum(row_piece * row_piece)
    row_half = row_full.astype(jnp.bfloat16)
    col_half = col_full.astype(jnp.bfloat16)
    rows_needed = jnp.take(row_half, local_rows, axis=0)
    cols_needed = jnp.take(col_half, local_cols, axis=0)
    gradient = (
        0.5
        / samples
        * (
            jnp.einsum("san,nsb->sab", rows_needed, right_cols, preferred_element_type=jnp.float32)
            + jnp.einsum("nsa,snb->sab", left_rows, cols_needed, preferred_element_type=jnp.float32)
        )
    )
    global_rows = row_index * band_blocks + local_rows
    global_cols = col_index * blocks + local_cols
    on_diag = (global_rows == global_cols).astype(jnp.float32) * is_live
    identity = jnp.eye(tile_edge, dtype=jnp.float32)
    diag_vals = jnp.diagonal(tiles_now, axis1=1, axis2=2)
    safe_diag = jnp.where(on_diag[:, None] > 0, diag_vals, 1.0)
    center = on_diag[:, None, None] * identity[None, :, :]
    gradient = gradient - center * (1.0 / safe_diag)[:, None, :]
    stepped = tiles_now - step_size * gradient
    shrunk = jnp.sign(stepped) * jnp.maximum(jnp.abs(stepped) - step_size * penalty, 0.0)
    updated = jnp.where(center > 0, stepped, shrunk) * is_live[:, None, None]
    change = updated - tiles_now
    log_terms = jnp.sum(on_diag[:, None] * jnp.log(safe_diag))
    abs_before = jnp.sum(jnp.abs(tiles_now) * (1.0 - center))
    inner = jnp.sum(gradient * change)
    change_sq = jnp.sum(change * change)
    abs_after = jnp.sum(jnp.abs(updated) * (1.0 - center))
    totals = lax.psum((log_terms, squares, abs_before, inner, change_sq, abs_after), ("row", "col"))
    smooth = -totals[0] + totals[1] / (2.0 * samples)
    objective = smooth + penalty * totals[2]
    model_bound = smooth + totals[3] + totals[4] / (2.0 * step_size) + penalty * totals[5]
    return (updated[None, None], jnp.stack([objective, model_bound]))


def solution(mesh):
    placed = (
        P(None, "col"),
        P("row", "col", None, None, None),
        P("row", "col", None),
        P("row", "col", None),
        P("row", "col"),
    )
    return jax.shard_map(
        local,
        mesh=mesh,
        in_specs=placed,
        out_specs=(P("row", "col", None, None, None), P()),
        check_vma=False,
    )
```

profile of v0, /device:TPU:1, one launch (start us, length us, event | category | flops | bytes accessed | tf_op | source)
XLA Modules:
  0.0 652.1 jit_solution(15431277311184653626)
XLA Ops:
  7.2 3.3 copy.21
  10.6 3.1 broadcast_select_fusion.3
  14.5 3.3 copy.22
  17.8 3.0 gather_fusion
  20.8 5.4 bitcast_multiply_fusion
  26.2 10.2 %fusion.15 = f32[10,512,384]{2,1,0:T(8,128)} fusion(f32[10,512,512]{2,1,0:T(8,128)S(1)} %bitcast_multiply_fusion, bf16[10,384,512]{2,1,0:T(8,128)(2,1)} %gather_fusion, pred[10]{0:T(512)(128)(4,1)S(1)} %get-tuple-element.22), kind=kOutput, calls=%fused_computation.28 | convolution fusion | flops 2017853440 | bytes 22282250 | tf_op jit(solution)/shard_map/sab,nsb->san/dot_general | solution.py:44
  36.5 21.6 %fusion.4 = f32[14,512,384]{2,0,1:T(8,128)} fusion(f32[10,512,384]{2,1,0:T(8,128)} %fusion.15, f32[10]{0:T(128)S(1)} %compare_convert_fusion.1, s32[10]{0:T(128)S(1)} %bitcast.53), kind=kOutput, calls=%fused_computation.12 | convolution fusion | flops 330301728 | bytes 18874448 | tf_op jit(solution)/shard_map/sr,san->ran/dot_general | solution.py:47
  58.1 12.2 %copy.24 = f32[14,512,384]{2,1,0:T(8,128)} copy(f32[14,512,384]{2,0,1:T(8,128)} %fusion.4) | data formatting | bytes 22020096 | tf_op jit(solution)/shard_map/sr,san->ran/dot_general | solution.py:47
  70.3 61.0 %copy.31 = f32[10,512,512]{0,2,1:T(8,128)} copy(f32[10,512,512]{2,1,0:T(8,128)} %copy-done) | data formatting | bytes 20971520 | tf_op jit(solution)/shard_map/mul | solution.py:28
  131.3 5.6 gather_fusion.4
  138.8 37.0 %all-reduce.8.cloned.1.call-done = (bf16[384,3584]{0,1:T(8,128)(2,1)}, bf16[384,3584]{0,1:T(8,128)(2,1)}) async-done(((bf16[384,3584]{0,1:T(8,128)(2,1)}, bf16[384,3584]{0,1:T(8,128)(2,1)}), (bf16[384,3584]{0,1:T(8,128)(2,1)}, bf16[384,3584]{0,1:T(8,128)(2,1)})) %all-reduce.8.cloned.1.call-update) | async-done | bytes 5505040 | tf_op jit(solution)/shard_map/psum | solution.py:12
  175.8 5.5 pad_maximum_fusion
  181.3 8.3 %copy.27 = bf16[384,14,512]{2,0,1:T(8,128)(2,1)} copy(bf16[384,14,512]{0,2,1:T(8,128)(2,1)} %bitcast.52) | data formatting | bytes 11010048 | tf_op jit(solution)/shard_map/reshape | solution.py:35
  189.6 5.6 gather_fusion.2
  195.2 7.4 %fusion.11 = f32[10,384,512]{2,1,0:T(8,128)S(1)} fusion(f32[10,512,512]{2,1,0:T(8,128)} %copy-done, bf16[10,384,512]{2,1,0:T(8,128)(2,1)} %gather_fusion.2, pred[10]{0:T(512)(128)(4,1)S(1)} %get-tuple-element.21), kind=kOutput, calls=%fused_computation.24 | convolution fusion | flops 2017853440 | bytes 22282250 | tf_op jit(solution)/shard_map/nsa,sab->snb/dot_general | solution.py:48
  202.6 13.8 %fusion.2 = f32[7,384,512]{2,0,1:T(8,128)} fusion(f32[10,384,512]{2,1,0:T(8,128)S(1)} %fusion.11, f32[10]{0:T(128)S(1)} %compare_convert_fusion.1, s32[10]{0:T(128)S(1)} %bitcast.54), kind=kOutput, calls=%fused_computation.10 | convolution fusion | flops 165150864 | bytes 13369424 | tf_op jit(solution)/shard_map/sb,snt->bnt/dot_general | solution.py:51
  216.4 231.5 %all-reduce.9 = bf16[7,384,512]{2,0,1:T(8,128)(2,1)} all-reduce(f32[7,384,512]{2,0,1:T(8,128)} %fusion.2), channel_id=1, replica_groups=mesh['row'=8,'col'=16] {'row'}, use_global_device_ids=true, to_apply=%region_3.4 | all-reduce | flops 1376256 | bytes 8257536 | tf_op jit(solution)/shard_map/psum | solution.py:54
  453.8 10.4 %fusion.9 = f32[10,512,512]{2,1,0:T(8,128)} fusion(bf16[10,384,512]{2,1,0:T(8,128)(2,1)} %gather_fusion.3, pred[10]{0:T(512)(128)(4,1)S(1)} %get-tuple-element.22, bf16[10,384,512]{2,1,0:T(8,128)(2,1)} %gather_fusion.2, pred[10]{0:T(512)(128)(4,1)S(1)} %get-tuple-element.21), kind=kOutput, calls=%fused_computation.22 | convolution fusion | flops 2017198080 | bytes 18350100 | tf_op jit(solution)/shard_map/nsa,snb->sab/dot_general | solution.py:66
  464.2 67.7 %all-reduce.6.cloned.1.call-done = f32[14,512,384]{2,1,0:T(8,128)} async-done(((f32[14,512,384]{2,1,0:T(8,128)}), f32[14,512,384]{2,1,0:T(8,128)}) %all-reduce.6.cloned.1.call-update) | async-done | bytes 11010064 | tf_op jit(solution)/shard_map/psum | solution.py:53
  531.9 7.4 %convert_element_type.50 = bf16[14,512,384]{2,1,0:T(8,128)(2,1)} convert(f32[14,512,384]{2,1,0:T(8,128)} %all-reduce.6.cloned.1.call-done) | non-fusion elementwise | flops 2752512 | bytes 16515072 | tf_op jit(solution)/shard_map/convert_element_type | solution.py:57
  539.2 6.0 gather_fusion.1
  545.3 23.3 %fusion.7 = (f32[]{:T(128)}, f32[]{:T(128)}, f32[]{:T(128)}, f32[]{:T(128)}, f32[1,1,10,512,512]{4,3,2,1,0:T(8,128)}) fusion(f32[512,512]{1,0:T(8,128)S(1)} %copy-done.2, f32[10]{0:T(128)S(1)} %get-tuple-element.15, f32[10]{0:T(128)S(1)} %compare_convert_fusion.1, f32[10,512,512]{2,1,0:T(8,128)} %copy-done, f32[10,512]{1,0:T(8,128)S(1)} %copy.32, ...), kind=kOutput, calls=%fused_computation.15 | convolution fusion | flops 2087976960 | bytes 40390772 | tf_op jit(solution)/shard_map/san,nsb->sab/dot_general | solution.py:65
  568.6 4.7 multiply_reduce_fusion.2
  573.3 67.4 %all-reduce = (f32[]{:T(128)}, f32[]{:T(128)}, f32[]{:T(128)}, f32[]{:T(128)}, f32[]{:T(128)}, /*index=5*/f32[]{:T(128)}) all-reduce(f32[]{:T(128)} %get-tuple-element.19, f32[]{:T(128)} %multiply_reduce_fusion.2, f32[]{:T(128)} %get-tuple-element.3, f32[]{:T(128)} %get-tuple-element.4, ...), channel_id=1, replica_groups=mesh['row'=8,'col'=16] {'row','col'}, use_global_device_ids=true, to_apply=%region_5.6 | all-reduce | flops 6 | bytes 48 | tf_op jit(solution)/shard_map/psum | solution.py:86
  (27 shorter events, 8.6 us)
Async XLA Ops:
  7.2 168.6 %all-reduce.8.cloned.1.call-start = ((), (), s32[]{:S(2)}) async-start(), calls=%async_computation.1 | async-start | bytes 11010048 | tf_op jit(solution)/shard_map/psum | solution.py:12
  10.6 3.3 copy-start.1
  13.7 4.1 copy-start.4
  13.8 518.0 %all-reduce.6.cloned.1.call-start = ((), (), s32[]{:S(2)}) async-start(), calls=%async_computation | async-start | bytes 22020096 | tf_op jit(solution)/shard_map/psum | solution.py:53
  17.8 3.0 copy-start.3
  26.2 10.2 %copy-start = (f32[10,512,512]{2,1,0:T(8,128)}, f32[10,512,512]{2,1,0:T(8,128)S(1)}, u32[]{:S(2)}) copy-start(f32[10,512,512]{2,1,0:T(8,128)S(1)} %bitcast_multiply_fusion) | copy-start | bytes 31457284
  539.2 6.0 copy-start.2
Sparse Core Ops, SparseCore 0:
  13.9 161.8 all-reduce.7
  178.3 353.5 all-reduce.5
where the time goes:
time: 659 us; the launch traced here: 652 us
  blocking collectives  299 us (45%)
  local copies, waits for them, and re-layouts  114 us (17%)
  waiting for transfers between devices  105 us (16%)
  matrix products  86.7 us (13%)
  other arithmetic  28.5 us (4%)
  between operations  18.9 us (3%)
    psum x1, blocking collectives, local(): col_full = lax.psum(col_partial, 'row')  232 us
    psum x1, waiting for transfers between devices, local(): row_full = lax.psum(row_partial, 'col')  67.7 us
    psum x1, blocking collectives, local(): lax.psum((log_terms, squares, abs_before, inner, change_sq, abs_after), (...  67.4 us
    mul x1, local copies, waits for them, and re-layouts, local(): tiles_now = omega_tiles[0, 0] * is_live[:, None, None]  61 us
    psum x1, waiting for transfers between devices, spread(): return lax.psum(kept, axis)  37 us
    dot_general x1, matrix products, local(): jnp.einsum('san,nsb->sab', rows_needed, right_cols, preferred_element_typ...  23.3 us
    dot_general x1, matrix products, local(): jnp.einsum('sr,san->ran', pick_rows, row_terms, precision=lax.Precision.H...  21.6 us
    dot_general x1, matrix products, local(): jnp.einsum('sb,snt->bnt', pick_cols, col_terms, precision=lax.Precision.H...  13.8 us
  transfers between devices with their start and end apart: 2, of which 2 were waited for; matrix products, arithmetic and copies ran while one was open for 28% of the time, Pallas kernels for 0%

commit v1 on v0

v1 whole, which is shorter than its diff:
```python
import functools

import jax
import jax.numpy as jnp
from jax import lax
from jax.experimental import pallas as pl
from jax.experimental.pallas import tpu as pltpu
from jax.sharding import PartitionSpec as P

MESH = pl.DeviceIdType.MESH
F32 = jnp.float32
BF16 = jnp.bfloat16

STEP = 0.1
PENALTY = 0.3
THRESH = STEP * PENALTY

TILE = 512
BLK = 7
BAND = 14
SLOTS = 10
SCANS = 384

ROWS = BAND * TILE
HALF = ROWS // 2
ROW_LEN = (1152, 1152, 1280)
ROW_BASE = (0, 1152, 2304)
COLS = BLK * SCANS
COL_LEN = (896, 896, 896)
COL_BASE = (0, 896, 1792)
PIECE_BASE = (0, 144, 288)
OWN = HALF // 8
CHUNKS = 14
CH = SCANS // 2


class Place:
    def __init__(self):
        self.row = lax.axis_index("row")
        self.col = lax.axis_index("col")
        self.yl = self.row // 4
        self.z = self.row % 4
        self.x = self.col // 4
        self.yh = (self.col // 2) % 2
        self.core = self.col % 2
        self.bits = {
            "xa": ((self.x + 1) // 2) % 2,
            "xb": self.x // 2,
            "yh": self.yh,
            "za": ((self.z + 1) // 2) % 2,
            "zb": self.z // 2,
            "yl": self.yl,
            "core": self.core,
        }

    def at(self, x=None, yh=None, core=None, yl=None, z=None):
        x = self.x if x is None else x
        yh = self.yh if yh is None else yh
        core = self.core if core is None else core
        yl = self.yl if yl is None else yl
        z = self.z if z is None else z
        return (yl * 4 + z, x * 4 + yh * 2 + core)

    def partner(self, dim):
        if dim == "core":
            return self.at(core=1 - self.core)
        if dim == "yh":
            return self.at(yh=1 - self.yh)
        if dim == "yl":
            return self.at(yl=1 - self.yl)
        if dim == "xa":
            return self.at(x=self.x + 1 - 2 * (self.x % 2))
        if dim == "xb":
            return self.at(x=(self.x + 3 + 2 * (self.x % 2)) % 4)
        if dim == "za":
            return self.at(z=self.z + 1 - 2 * (self.z % 2))
        return self.at(z=(self.z + 3 + 2 * (self.z % 2)) % 4)


ROW_ORDERS = (("xa", "xb", "yh"), ("xb", "yh", "xa"), ("yh", "xa", "xb"))
COL_ORDERS = (("za", "zb", "yl"), ("zb", "yl", "za"), ("yl", "za", "zb"))


def greet(place, dims):
    barrier = pltpu.get_barrier_semaphore()
    for dim in dims:
        pl.semaphore_signal(barrier, inc=1, device_id=place.partner(dim), device_id_type=MESH)
    pl.semaphore_wait(barrier, len(dims))


def segments(place, base, length, dims):
    out = []
    start, n = base, length
    for dim in dims:
        n = n // 2
        bit = place.bits[dim]
        keep = pl.multiple_of(start + bit * n, 16)
        send = pl.multiple_of(start + (1 - bit) * n, 16)
        out.append((keep, send, n))
        start = keep
    return out


def block_of(n):
    for blk in (128, 112, 96, 80, 64, 48, 32, 16):
        if n % blk == 0:
            return blk
    return n


def add_rows(dst, dst_at, one, one_at, two, two_at, n):
    blk = block_of(n)

    def body(i, carry):
        o = i * blk
        a = one[pl.ds(pl.multiple_of(one_at + o, 16), blk), :].astype(F32)
        b = two[pl.ds(pl.multiple_of(two_at + o, 16), blk), :].astype(F32)
        dst[pl.ds(pl.multiple_of(dst_at + o, 16), blk), :] = (a + b).astype(dst.dtype)
        return carry

    lax.fori_loop(0, n // blk, body, 0)


def row_partial_kernel(rows_s, cols_s, meta_s, omega_ref, series_ref, out_ref, acc_ref):
    s = pl.program_id(0)

    @pl.when(s == 0)
    def _():
        def zero(i, carry):
            acc_ref[i] = jnp.zeros((TILE, SCANS), F32)
            return carry

        lax.fori_loop(0, BAND, zero, 0)

    @pl.when(s < meta_s[0])
    def _():
        half = omega_ref[0].astype(BF16)
        at = pl.multiple_of(cols_s[s] * TILE, TILE)
        panel = series_ref[:, pl.ds(at, TILE)]
        term = lax.dot_general(half, panel, (((1,), (1,)), ((), ())), preferred_element_type=F32)
        acc_ref[rows_s[s]] += term

    @pl.when(s == SLOTS - 1)
    def _():
        def cast(i, carry):
            out_ref[i] = acc_ref[i].astype(BF16)
            return carry

        lax.fori_loop(0, BAND, cast, 0)


def col_partial_kernel(rows_s, cols_s, meta_s, omega_ref, band_ref, out_ref, acc_ref):
    s = pl.program_id(0)

    @pl.when(s == 0)
    def _():
        def zero(i, carry):
            acc_ref[i] = jnp.zeros((SCANS, TILE), F32)
            return carry

        lax.fori_loop(0, BLK, zero, 0)

    @pl.when(s < meta_s[0])
    def _():
        half = omega_ref[0].astype(BF16)
        acc_ref[cols_s[s]] += jnp.dot(band_ref[0], half, preferred_element_type=F32)

    @pl.when(s == SLOTS - 1)
    def _():
        def cast(i, carry):
            out_ref[i] = acc_ref[i].astype(BF16)
            return carry

        lax.fori_loop(0, BLK, cast, 0)


def band_kernel(series, part, band, own, squares, sbuf, acc, recv_core, recv_st,
                ss_r, rs_r, ss_b, rs_b, ss_y, ss_s, rs_s, ls):
    place = Place()
    core = place.core
    xs = place.yl * 2 + place.z // 2
    ys = place.z % 2
    sign = 1 - 2 * core
    d = (sign * (place.x - xs) + 4) % 4
    source = jnp.logical_and(d == 0, place.yh == ys)
    follow = jnp.logical_not(source)
    onward = place.at(x=(place.x + sign + 4) % 4)
    sister = place.partner("core")
    across = place.partner("yh")

    greet(place, ("core", "xa", "xb", "yh"))

    keep0 = pl.multiple_of(core * HALF, 16)
    send0 = pl.multiple_of((1 - core) * HALF, 16)
    first = pltpu.make_async_remote_copy(
        part.at[pl.ds(send0, HALF)], recv_core, ss_r.at[9], rs_r.at[9], device_id=sister, device_id_type=MESH)
    first.start()
    mine = pltpu.make_async_copy(part.at[pl.ds(keep0, HALF)], acc, ls.at[0])
    mine.start()

    def slot(i, which):
        return band.at[which * BLK + i // 2, pl.ds((i % 2) * CH, CH), :]

    def native(i):
        return sbuf.at[:, pl.ds((i // 2) * TILE, TILE)].at[pl.ds((i % 2) * CH, CH), :]

    def to_next(src, i):
        return pltpu.make_async_remote_copy(src, slot(i, core), ss_b.at[i], rs_b.at[i],
                                            device_id=onward, device_id_type=MESH)

    def to_across(src, i):
        return pltpu.make_async_remote_copy(src, slot(i, core), ss_y.at[i], rs_b.at[i],
                                            device_id=across, device_id_type=MESH)

    def to_sister(src, i):
        return pltpu.make_async_remote_copy(src, slot(i, core), ss_s.at[i], rs_s.at[i],
                                            device_id=sister, device_id_type=MESH)

    def keep_native(i):
        return pltpu.make_async_copy(native(i), slot(i, core), ls.at[2 + i])

    load = pltpu.make_async_copy(series, sbuf, ls.at[1])

    @pl.when(source)
    def _():
        load.start()
        load.wait()

    def source_step(i):
        @pl.when(source)
        def _():
            to_next(native(i), i).start()
            to_across(native(i), i).start()
            to_sister(native(i), i).start()
            keep_native(i).start()

    def follow_step(i):
        @pl.when(follow)
        def _():
            to_next(slot(i, core), i).wait_recv()

            @pl.when(d < 3)
            def _():
                to_next(slot(i, core), i).start()

            to_sister(slot(i, core), i).start()

    segs = [segments(place, ROW_BASE[o], ROW_LEN[o], ROW_ORDERS[o]) for o in range(3)]
    recv_at = []
    at = 0
    for o in range(3):
        line = []
        for keep, send, n in segs[o]:
            line.append(at)
            at += n
        recv_at.append(line)

    def exchange(o, j):
        keep, send, n = segs[o][j]
        return pltpu.make_async_remote_copy(
            acc.at[pl.ds(send, n)], recv_st.at[pl.ds(recv_at[o][j], n)], ss_r.at[o * 3 + j], rs_r.at[o * 3 + j],
            device_id=place.partner(ROW_ORDERS[o][j]), device_id_type=MESH)

    source_step(0)
    source_step(1)
    mine.wait()
    first.wait_recv()
    add_rows(acc, 0, acc, 0, recv_core, 0, HALF)
    for o in range(3):
        exchange(o, 0).start()
    for i in range(0, 4):
        source_step(i + 2)
        follow_step(i)
    for o in range(3):
        keep, send, n = segs[o][0]
        exchange(o, 0).wait_recv()
        add_rows(acc, keep, acc, keep, recv_st, recv_at[o][0], n)
        exchange(o, 1).start()
    for i in range(4, 8):
        source_step(i + 2)
        follow_step(i)
    for o in range(3):
        keep, send, n = segs[o][1]
        exchange(o, 1).wait_recv()
        add_rows(acc, keep, acc, keep, recv_st, recv_at[o][1], n)
        exchange(o, 2).start()
    for i in range(8, CHUNKS):
        if i + 2 < CHUNKS:
            source_step(i + 2)
        follow_step(i)
    total = jnp.zeros((8, SCANS), F32)
    for o in range(3):
        keep, send, n = segs[o][2]
        exchange(o, 2).wait_recv()

        def body(i, total, o=o, keep=keep):
            a = acc[pl.ds(pl.multiple_of(keep + i * 16, 16), 16), :].astype(F32)
            b = recv_st[pl.ds(pl.multiple_of(recv_at[o][2] + i * 16, 16), 16), :].astype(F32)
            c = a + b
            own[pl.ds(pl.multiple_of(PIECE_BASE[o] + i * 16, 16), 16), :] = c.astype(BF16)
            c2 = c * c
            return total + c2[:8] + c2[8:]

        total = lax.fori_loop(0, n // 16, body, total)
    squares[...] = total
    for i in range(CHUNKS):
        to_sister(slot(i, 1 - core), i).wait_recv()
        to_sister(slot(i, core), i).wait_send()

        @pl.when(d < 3)
        def _():
            to_next(slot(i, core), i).wait_send()

        @pl.when(source)
        def _():
            to_across(native(i), i).wait_send()
            keep_native(i).wait()
    first.wait_send()
    for o in range(3):
        for j in range(3):
            exchange(o, j).wait_send()


def sums_kernel(own, colpart, rowhalf, colhalf, acc, recv, fin, ss_r, rs_r, ss_s, rs_s, ss_c, rs_c, ls):
    place = Place()
    core = place.core
    sister = place.partner("core")
    greet(place, ("core", "xa", "xb", "yh", "za", "zb", "yl"))

    csegs = [segments(place, COL_BASE[o], COL_LEN[o], COL_ORDERS[o]) for o in range(3)]
    recv_at = []
    at = 0
    for o in range(3):
        line = []
        for keep, send, n in csegs[o]:
            line.append(at)
            at += n
        recv_at.append(line)

    def exchange(o, j):
        keep, send, n = csegs[o][j]
        src = colpart if j == 0 else acc
        return pltpu.make_async_remote_copy(
            src.at[pl.ds(send, n)], recv.at[pl.ds(recv_at[o][j], n)], ss_c.at[o * 6 + j], rs_c.at[o * 6 + j],
            device_id=place.partner(COL_ORDERS[o][j]), device_id_type=MESH)

    rsegs = [segments(place, ROW_BASE[o], ROW_LEN[o], ROW_ORDERS[o]) for o in range(3)]
    home = core * HALF
    away = (1 - core) * HALF

    def row_at(which, start, n):
        return rowhalf.at[pl.ds(pl.multiple_of(which + start, 16), n)]

    def row_gather(o, j):
        keep, send, n = rsegs[o][j]
        src = own.at[pl.ds(PIECE_BASE[o], n)] if j == 2 else row_at(home, keep, n)
        return pltpu.make_async_remote_copy(
            src, row_at(home, keep, n), ss_r.at[o * 3 + j], rs_r.at[o * 3 + j],
            device_id=place.partner(ROW_ORDERS[o][j]), device_id_type=MESH)

    def row_arrived(o, j):
        keep, send, n = rsegs[o][j]
        return pltpu.make_async_remote_copy(
            row_at(home, send, n), row_at(home, send, n), ss_r.at[o * 3 + j], rs_r.at[o * 3 + j],
            device_id=place.partner(ROW_ORDERS[o][j]), device_id_type=MESH)

    def row_local(o):
        keep, send, n = rsegs[o][2]
        return pltpu.make_async_copy(own.at[pl.ds(PIECE_BASE[o], n)], row_at(home, keep, n), ls.at[o])

    def row_share(o, j, which=None):
        if j == 3:
            keep, send, n = rsegs[o][2]
            src = own.at[pl.ds(PIECE_BASE[o], n)]
            start = keep
        else:
            keep, send, n = rsegs[o][j]
            src = row_at(home, send, n)
            start = send
        return pltpu.make_async_remote_copy(
            src, row_at(home, start, n), ss_s.at[o * 4 + j], rs_s.at[o * 4 + j], device_id=sister, device_id_type=MESH)

    def col_at(start, n):
        return colhalf.at[pl.ds(start, n)]

    def col_gather(o, j):
        keep, send, n = csegs[o][j]
        src = fin.at[pl.ds(o * 112, n)] if j == 2 else col_at(keep, n)
        return pltpu.make_async_remote_copy(
            src, col_at(keep, n), ss_c.at[o * 6 + 3 + j], rs_c.at[o * 6 + 3 + j],
            device_id=place.partner(COL_ORDERS[o][j]), device_id_type=MESH)

    def col_local(o):
        keep, send, n = csegs[o][2]
        return pltpu.make_async_copy(fin.at[pl.ds(o * 112, n)], col_at(keep, n), ls.at[3 + o])

    for o in range(3):
        exchange(o, 0).start()
    for o in range(3):
        row_gather(o, 2).start()
        row_local(o).start()
        row_share(o, 3).start()
    for o in range(3):
        keep, send, n = csegs[o][0]
        exchange(o, 0).wait_recv()
        add_rows(acc, keep, colpart, keep, recv, recv_at[o][0], n)
        exchange(o, 1).start()
    for o in range(3):
        row_local(o).wait()
        row_arrived(o, 2).wait_recv()
        row_gather(o, 1).start()
        row_share(o, 2).start()
    for o in range(3):
        keep, send, n = csegs[o][1]
        exchange(o, 1).wait_recv()
        add_rows(acc, keep, acc, keep, recv, recv_at[o][1], n)
        exchange(o, 2).start()
    for o in range(3):
        keep, send, n = csegs[o][2]
        exchange(o, 2).wait_recv()
        add_rows(fin, o * 112, acc, keep, recv, recv_at[o][2], n)
        col_gather(o, 2).start()
        col_local(o).start()
    for o in range(3):
        row_arrived(o, 1).wait_recv()
        row_gather(o, 0).start()
        row_share(o, 1).start()
    for j in (2, 1):
        for o in range(3):
            if j == 2:
                col_local(o).wait()
            col_gather(o, j).wait_recv()
            col_gather(o, j - 1).start()
    for o in range(3):
        row_arrived(o, 0).wait_recv()
        row_share(o, 0).start()
    for o in range(3):
        col_gather(o, 0).wait_recv()
    for o in range(3):
        for j in range(4):
            row_share(o, j).wait_recv()
            row_share(o, j).wait_send()
        for j in range(3):
            row_gather(o, j).wait_send()
            exchange(o, j).wait_send()
            col_gather(o, j).wait_send()


def update_kernel(rows_s, cols_s, meta_s, omega_ref, rowhalf_ref, band_ref, series_ref, colhalf_ref,
                  out_ref, sums_ref, grad_ref, acc_ref, diag_ref):
    s = pl.program_id(0)
    live = s < meta_s[0]

    @pl.when(s == 0)
    def _():
        acc_ref[...] = jnp.zeros_like(acc_ref)
        diag_ref[...] = jnp.zeros_like(diag_ref)

    @pl.when(jnp.logical_not(live))
    def _():
        out_ref[0] = jnp.zeros((TILE, TILE), F32)

    @pl.when(live)
    def _():
        grad_ref[...] = (0.5 / SCANS) * (
            jnp.dot(rowhalf_ref[0], series_ref[...], preferred_element_type=F32)
            + lax.dot_general(band_ref[0], colhalf_ref[0], (((0,), (0,)), ((), ())), preferred_element_type=F32)
        )
        blk = 32

        def fold(v):
            return v[0:8] + v[8:16] + v[16:24] + v[24:32]

        def body(i, carry):
            before, inner, moved, after = carry
            at = pl.ds(pl.multiple_of(i * blk, blk), blk)
            now = omega_ref[0, at, :]
            grad = grad_ref[at, :]
            stepped = now - STEP * grad
            updated = stepped - jnp.clip(stepped, -THRESH, THRESH)
            change = updated - now
            out_ref[0, at, :] = updated
            return (before + fold(jnp.abs(now)), inner + fold(grad * change), moved + fold(change * change),
                    after + fold(jnp.abs(updated)))

        zero = jnp.zeros((8, TILE), F32)
        before, inner, moved, after = lax.fori_loop(0, TILE // blk, body, (zero, zero, zero, zero))
        acc_ref[0] += before
        acc_ref[1] += inner
        acc_ref[2] += moved
        acc_ref[3] += after

        @pl.when(meta_s[1] + rows_s[s] == meta_s[2] + cols_s[s])
        def _():
            mask = lax.broadcasted_iota(jnp.int32, (128, 128), 0) == lax.broadcasted_iota(jnp.int32, (128, 128), 1)
            for q in range(TILE // 128):
                at = slice(q * 128, (q + 1) * 128)

                def pick(v):
                    return jnp.sum(jnp.where(mask, v, 0.0), axis=0, keepdims=True)

                now = pick(omega_ref[0, at, at])
                plain = pick(grad_ref[at, at])
                shrunk = out_ref[0, at, at]
                old = pick(shrunk)
                grad = plain - 1.0 / now
                stepped = now - STEP * grad
                change = stepped - now
                old_change = old - now
                out_ref[0, at, at] = jnp.where(mask, stepped, shrunk)
                diag_ref[0:1] += jnp.log(now)
                diag_ref[1:2] -= jnp.abs(now)
                diag_ref[2:3] += grad * change - plain * old_change
                diag_ref[3:4] += change * change - old_change * old_change
                diag_ref[4:5] -= jnp.abs(old)

    @pl.when(s == SLOTS - 1)
    def _():
        sums_ref[0:1] = diag_ref[0:1]
        for t in range(4):
            v = acc_ref[t]
            v = v[:, 0:128] + v[:, 128:256] + v[:, 256:384] + v[:, 384:512]
            sums_ref[1 + t:2 + t] = jnp.sum(v, axis=0, keepdims=True) + diag_ref[1 + t:2 + t]
        sums_ref[5:8] = jnp.zeros((3, 128), F32)


def total_kernel(sums, squares, out, vec, recv_a, recv_b, ss, rs):
    place = Place()
    row, col = place.row, place.col
    barrier = pltpu.get_barrier_semaphore()
    for k in range(1, 16):
        pl.semaphore_signal(barrier, inc=1, device_id=(row, (col + k) % 16), device_id_type=MESH)
    for k in range(1, 8):
        pl.semaphore_signal(barrier, inc=1, device_id=((row + k) % 8, col), device_id_type=MESH)
    v = squares[...]
    v = jnp.sum(v, axis=0, keepdims=True)
    v = v[:, 0:128] + v[:, 128:256] + v[:, 256:384]
    spot = lax.broadcasted_iota(jnp.int32, (8, 128), 0) == 5
    vec[0] = sums[...] + jnp.where(spot, jnp.broadcast_to(v, (8, 128)), 0.0)
    pl.semaphore_wait(barrier, 22)

    def across(k):
        return pltpu.make_async_remote_copy(vec.at[0], recv_a.at[col], ss.at[k - 1], rs.at[k - 1],
                                            device_id=(row, (col + k) % 16), device_id_type=MESH)

    def down(k):
        return pltpu.make_async_remote_copy(vec.at[1], recv_b.at[row], ss.at[14 + k], rs.at[14 + k],
                                            device_id=((row + k) % 8, col), device_id_type=MESH)

    for k in range(1, 16):
        across(k).start()
    recv_a[col] = vec[0]
    for k in range(1, 16):
        across(k).wait_recv()
    total = recv_a[0]
    for k in range(1, 16):
        total = total + recv_a[k]
    vec[1] = total
    for k in range(1, 8):
        down(k).start()
    recv_b[row] = total
    for k in range(1, 8):
        down(k).wait_recv()
    total = recv_b[0]
    for k in range(1, 8):
        total = total + recv_b[k]
    s = jnp.sum(total, axis=1, keepdims=True)
    smooth = -s[0:1] + s[5:6] / (2.0 * SCANS)
    objective = smooth + PENALTY * s[1:2]
    bound = smooth + s[2:3] + s[3:4] / (2.0 * STEP) + PENALTY * s[4:5]
    lane = lax.broadcasted_iota(jnp.int32, (1, 128), 1)
    out[...] = jnp.where(lane == 0, objective, bound)
    for k in range(1, 16):
        across(k).wait_send()
    for k in range(1, 8):
        down(k).wait_send()


def local(series, omega_tiles, tile_row, tile_col, tile_count):
    omega = omega_tiles[0, 0]
    rows_s = tile_row[0, 0]
    cols_s = tile_col[0, 0]
    meta = jnp.stack([tile_count[0, 0], lax.axis_index("row") * BAND, lax.axis_index("col") * BLK]).astype(jnp.int32)
    big = 60 << 20
    vmem = pl.BlockSpec(memory_space=pltpu.VMEM)
    hbm = pl.BlockSpec(memory_space=pl.ANY)

    def plain(**kw):
        return pltpu.CompilerParams(vmem_limit_bytes=big, **kw)

    row_part = pl.pallas_call(
        row_partial_kernel,
        out_shape=jax.ShapeDtypeStruct((BAND, TILE, SCANS), BF16),
        grid_spec=pltpu.PrefetchScalarGridSpec(
            num_scalar_prefetch=3, grid=(SLOTS,),
            in_specs=[pl.BlockSpec((1, TILE, TILE), lambda s, *_: (s, 0, 0)),
                      pl.BlockSpec((SCANS, BLK * TILE), lambda s, *_: (0, 0))],
            out_specs=pl.BlockSpec((BAND, TILE, SCANS), lambda s, *_: (0, 0, 0)),
            scratch_shapes=[pltpu.VMEM((BAND, TILE, SCANS), F32)]),
        compiler_params=plain(), name="row_partial",
    )(rows_s, cols_s, meta, omega, series)

    band, own, squares = pl.pallas_call(
        band_kernel,
        out_shape=(jax.ShapeDtypeStruct((BAND, SCANS, TILE), BF16),
                   jax.ShapeDtypeStruct((OWN, SCANS), BF16),
                   jax.ShapeDtypeStruct((8, SCANS), F32)),
        in_specs=[hbm, hbm], out_specs=(hbm, vmem, vmem),
        scratch_shapes=[pltpu.VMEM((SCANS, BLK * TILE), BF16), pltpu.VMEM((HALF, SCANS), BF16),
                        pltpu.VMEM((HALF, SCANS), BF16), pltpu.VMEM((HALF * 7 // 8, SCANS), BF16),
                        pltpu.SemaphoreType.DMA((10,)), pltpu.SemaphoreType.DMA((10,)),
                        pltpu.SemaphoreType.DMA((CHUNKS,)), pltpu.SemaphoreType.DMA((CHUNKS,)),
                        pltpu.SemaphoreType.DMA((CHUNKS,)),
                        pltpu.SemaphoreType.DMA((CHUNKS,)), pltpu.SemaphoreType.DMA((CHUNKS,)),
                        pltpu.SemaphoreType.DMA((CHUNKS + 2,))],
        compiler_params=plain(collective_id=0, has_side_effects=True), name="band",
    )(series, row_part.reshape(ROWS, SCANS))

    col_part = pl.pallas_call(
        col_partial_kernel,
        out_shape=jax.ShapeDtypeStruct((BLK, SCANS, TILE), BF16),
        grid_spec=pltpu.PrefetchScalarGridSpec(
            num_scalar_prefetch=3, grid=(SLOTS,),
            in_specs=[pl.BlockSpec((1, TILE, TILE), lambda s, *_: (s, 0, 0)),
                      pl.BlockSpec((1, SCANS, TILE), lambda s, r, c, m: (r[s], 0, 0))],
            out_specs=pl.BlockSpec((BLK, SCANS, TILE), lambda s, *_: (0, 0, 0)),
            scratch_shapes=[pltpu.VMEM((BLK, SCANS, TILE), F32)]),
        compiler_params=plain(), name="col_partial",
    )(rows_s, cols_s, meta, omega, band)

    row_half, col_half = pl.pallas_call(
        sums_kernel,
        out_shape=(jax.ShapeDtypeStruct((ROWS, SCANS), BF16), jax.ShapeDtypeStruct((COLS, TILE), BF16)),
        in_specs=[vmem, vmem], out_specs=(hbm, hbm),
        scratch_shapes=[pltpu.VMEM((COLS, TILE), BF16), pltpu.VMEM((COLS * 7 // 8, TILE), BF16),
                        pltpu.VMEM((COLS // 8, TILE), BF16),
                        pltpu.SemaphoreType.DMA((9,)), pltpu.SemaphoreType.DMA((9,)),
                        pltpu.SemaphoreType.DMA((12,)), pltpu.SemaphoreType.DMA((12,)),
                        pltpu.SemaphoreType.DMA((18,)), pltpu.SemaphoreType.DMA((18,)),
                        pltpu.SemaphoreType.DMA((6,))],
        compiler_params=plain(collective_id=1, has_side_effects=True), name="sums",
    )(own, col_part.reshape(COLS, TILE))

    omega_next, sums = pl.pallas_call(
        update_kernel,
        out_shape=(jax.ShapeDtypeStruct((SLOTS, TILE, TILE), F32), jax.ShapeDtypeStruct((8, 128), F32)),
        grid_spec=pltpu.PrefetchScalarGridSpec(
            num_scalar_prefetch=3, grid=(SLOTS,),
            in_specs=[pl.BlockSpec((1, TILE, TILE), lambda s, *_: (s, 0, 0)),
                      pl.BlockSpec((1, TILE, SCANS), lambda s, r, c, m: (r[s], 0, 0)),
                      pl.BlockSpec((1, SCANS, TILE), lambda s, r, c, m: (r[s], 0, 0)),
                      pl.BlockSpec((SCANS, TILE), lambda s, r, c, m: (0, c[s])),
                      pl.BlockSpec((1, SCANS, TILE), lambda s, r, c, m: (c[s], 0, 0))],
            out_specs=(pl.BlockSpec((1, TILE, TILE), lambda s, *_: (s, 0, 0)),
                       pl.BlockSpec((8, 128), lambda s, *_: (0, 0))),
            scratch_shapes=[pltpu.VMEM((TILE, TILE), F32), pltpu.VMEM((4, 8, TILE), F32), pltpu.VMEM((8, 128), F32)]),
        compiler_params=plain(), name="update",
    )(rows_s, cols_s, meta, omega, row_half.reshape(BAND, TILE, SCANS), band, series, col_half.reshape(BLK, SCANS, TILE))

    values = pl.pallas_call(
        total_kernel,
        out_shape=jax.ShapeDtypeStruct((1, 128), F32),
        in_specs=[vmem, vmem], out_specs=vmem,
        scratch_shapes=[pltpu.VMEM((2, 8, 128), F32), pltpu.VMEM((16, 8, 128), F32), pltpu.VMEM((8, 8, 128), F32),
                        pltpu.SemaphoreType.DMA((22,)), pltpu.SemaphoreType.DMA((22,))],
        compiler_params=plain(collective_id=2, has_side_effects=True), name="total",
    )(sums, squares)
    return omega_next[None, None], values[0, :2]


def solution(mesh):
    placed = (
        P(None, "col"),
        P("row", "col", None, None, None),
        P("row", "col", None),
        P("row", "col", None),
        P("row", "col"),
    )
    return jax.shard_map(
        local,
        mesh=mesh,
        in_specs=placed,
        out_specs=(P("row", "col", None, None, None), P()),
        check_vma=False,
    )
```

time: 659 us -> 229 us (0.35); the launches traced: 652 us -> 229 us
  blocking collectives: 299 us -> 0 us
  Pallas kernels: 0 us -> 226 us
  local copies, waits for them, and re-layouts: 114 us -> 1.11 us
  waiting for transfers between devices: 105 us -> 0 us
  matrix products: 86.7 us -> 0 us
  other arithmetic: 28.5 us -> 0.65 us
  between operations: 18.9 us -> 1.31 us
    psum x2 -> x0, blocking collectives: 299 us -> none  [the longest x1 232 us: local(): col_full = lax.psum(col_partial, 'row')]
    pallas_call x0 -> x6, Pallas kernels: none -> 226 us  [the longest x1 84.5 us: local(): pl.pallas_call(band_kernel, out_shape=(jax.ShapeDtypeStruct((BAND, SCANS,...]
    psum x2 -> x0, waiting for transfers between devices: 105 us -> none  [the longest x1 67.7 us: local(): row_full = lax.psum(row_partial, 'col')]
    dot_general x6 -> x0, matrix products: 86.7 us -> none  [the longest x1 23.3 us: local(): jnp.einsum('san,nsb->sab', rows_needed, right_cols, preferred_element_typ...]
    mul x1 -> x0, local copies, waits for them, and re-layouts: 61 us -> none  [local(): tiles_now = omega_tiles[0, 0] * is_live[:, None, None]]
    gather x5 -> x0, local copies, waits for them, and re-layouts: 23.1 us -> none  [the longest x1 6.04 us: local(): rows_needed = jnp.take(row_half, local_rows, axis=0)]
    dot_general x1 -> x0, local copies, waits for them, and re-layouts: 12.2 us -> none  [local(): jnp.einsum('sr,san->ran', pick_rows, row_terms, precision=lax.Precision.H...]
    reshape x2 -> x0, local copies, waits for them, and re-layouts: 11.6 us -> none  [the longest x1 8.29 us: local(): band_split = band_panels.reshape(samples, band_blocks, tile_edge)]
  transfers between devices with their start and end apart: 2 -> 0, of which waited for: 2 -> 0; matrix products, arithmetic and copies ran while one was open for 28% -> 0% of each run, Pallas kernels for 0% -> 0%
where the time goes in v1:
time: 229 us
  Pallas kernels  226 us (99%)
    pallas_call x1, Pallas kernels, local(): pl.pallas_call(band_kernel, out_shape=(jax.ShapeDtypeStruct((BAND, SCANS,...  84.5 us
    pallas_call x1, Pallas kernels, local(): pl.pallas_call(sums_kernel, out_shape=(jax.ShapeDtypeStruct((ROWS, SCANS)...  81 us
    pallas_call x1, Pallas kernels, local(): pl.pallas_call(update_kernel, out_shape=(jax.ShapeDtypeStruct((SLOTS, TIL...  19.2 us
    pallas_call x1, Pallas kernels, local(): pl.pallas_call(total_kernel, out_shape=jax.ShapeDtypeStruct((1, 128), F32...  14.9 us
    pallas_call x1, Pallas kernels, local(): pl.pallas_call(row_partial_kernel, out_shape=jax.ShapeDtypeStruct((BAND,...  14.2 us
    pallas_call x1, Pallas kernels, local(): pl.pallas_call(col_partial_kernel, out_shape=jax.ShapeDtypeStruct((BLK, S...  11.8 us

profile of v1, /device:TPU:1, one launch (start us, length us, event | category | flops | bytes accessed | tf_op | source)
XLA Modules:
  0.0 228.7 jit_solution(17403061767376063932)
XLA Ops:
  1.3 0.6 pad_add_fusion.meta_s
  1.9 14.2 %row_partial.1 = bf16[14,512,384]{2,1,0:T(8,128)(2,1)} custom-call(s32[10]{0:T(128)} %bitcast.21, s32[10]{0:T(128)} %bitcast.24, s32[3]{0:T(128)} %pad_add_fusion.meta_s, f32[10,512,512]{2,1,0:T(8,128)} %bitcast.14, bf16[384,3584]{1,0:T(8,128)(2,1)} %series_ref.3), custom_call_target="tpu_custom_call" | custom-call | tf_op jit(solution)/shard_map/row_partial/pallas_call | solution.py:591
  16.2 84.5 %band.1 = (bf16[14,384,512]{2,1,0:T(8,128)(2,1)}, bf16[448,384]{1,0:T(8,128)(2,1)}, f32[8,384]{1,0:T(8,128)}) custom-call(bf16[384,3584]{1,0:T(8,128)(2,1)} %series_ref.3, bf16[7168,384]{1,0:T(8,128)(2,1)} %bitcast.17), custom_call_target="tpu_custom_call" | custom-call | tf_op jit(solution)/shard_map/band/pallas_call | solution.py:603
  100.6 11.8 %col_partial.1 = bf16[7,384,512]{2,1,0:T(8,128)(2,1)} custom-call(s32[10]{0:T(128)} %bitcast.22, s32[10]{0:T(128)} %bitcast.25, s32[3]{0:T(128)} %pad_add_fusion.meta_s, f32[10,512,512]{2,1,0:T(8,128)} %bitcast.15, bf16[14,384,512]{2,1,0:T(8,128)(2,1)} %get-tuple-element.10.band_ref), custom_call_target="tpu_custom_call" | custom-call | tf_op jit(solution)/shard_map/col_partial/pallas_call | solution.py:619
  112.5 81.0 %sums.1 = (bf16[7168,384]{1,0:T(8,128)(2,1)}, bf16[2688,512]{1,0:T(8,128)(2,1)}) custom-call(bf16[448,384]{1,0:T(8,128)(2,1)} %get-tuple-element.9.own, bf16[2688,512]{1,0:T(8,128)(2,1)} %bitcast.18), custom_call_target="tpu_custom_call" | custom-call | tf_op jit(solution)/shard_map/sums/pallas_call | solution.py:631
  193.5 19.2 %update.1 = (f32[10,512,512]{2,1,0:T(8,128)}, f32[8,128]{1,0:T(8,128)}) custom-call(s32[10]{0:T(128)} %bitcast.23, s32[10]{0:T(128)} %bitcast.26, s32[3]{0:T(128)} %pad_add_fusion.meta_s, f32[10,512,512]{2,1,0:T(8,128)} %bitcast.16, bf16[14,512,384]{2,1,0:T(8,128)(2,1)} %bitcast.19, bf16[14,384,512]{2,1,0:T(8,128)(2,1)} %get-tuple-element.10.band_ref, ...), custom_call_target="tpu_custom_call" | custom-call | tf_op jit(solution)/shard_map/update/pallas_call | solution.py:644
  212.7 14.9 %total.1 = f32[1,128]{1,0:T(1,128)} custom-call(f32[8,128]{1,0:T(8,128)} %get-tuple-element.14.sums, f32[8,384]{1,0:T(8,128)} %get-tuple-element.15.squares), custom_call_target="tpu_custom_call" | custom-call | tf_op jit(solution)/shard_map/total/pallas_call | solution.py:660
  227.6 1.1 slice_bitcast_fusion

commit v2 on v1

v2 whole, which is shorter than its diff:
```python
import functools

import jax
import jax.numpy as jnp
from jax import lax
from jax.experimental import pallas as pl
from jax.experimental.pallas import tpu as pltpu
from jax.sharding import PartitionSpec as P

MESH = pl.DeviceIdType.MESH
F32 = jnp.float32
BF16 = jnp.bfloat16

STEP = 0.1
PENALTY = 0.3
THRESH = STEP * PENALTY

TILE = 512
BLK = 7
BAND = 14
SLOTS = 10
SCANS = 384

ROWS = BAND * TILE
HALF = ROWS // 2
ROW_LEN = (1152, 1152, 1280)
COLS = BLK * SCANS
COL_LEN = (640, 640, 640, 768)
SPLIT = 4
CHUNKS = BLK * SPLIT
CH = SCANS // SPLIT


def bases(lengths):
    out, at = [], 0
    for n in lengths:
        out.append(at)
        at += n
    return out


ROW_BASE = bases(ROW_LEN)
COL_BASE = bases(COL_LEN)
ROW_FIN = bases([n // 8 for n in ROW_LEN])
COL_FIN = bases([n // 8 for n in COL_LEN])
RCH = len(ROW_LEN)
CCH = len(COL_LEN)


class Place:
    def __init__(self):
        self.row = lax.axis_index("row")
        self.col = lax.axis_index("col")
        self.yl = self.row // 4
        self.z = self.row % 4
        self.x = self.col // 4
        self.yh = (self.col // 2) % 2
        self.core = self.col % 2
        self.bits = {
            "xa": ((self.x + 1) // 2) % 2,
            "xb": self.x // 2,
            "yh": self.yh,
            "za": ((self.z + 1) // 2) % 2,
            "zb": self.z // 2,
            "yl": self.yl,
            "core": self.core,
        }

    def at(self, x=None, yh=None, core=None, yl=None, z=None):
        x = self.x if x is None else x
        yh = self.yh if yh is None else yh
        core = self.core if core is None else core
        yl = self.yl if yl is None else yl
        z = self.z if z is None else z
        return (yl * 4 + z, x * 4 + yh * 2 + core)

    def partner(self, dim):
        if dim == "core":
            return self.at(core=1 - self.core)
        if dim == "yh":
            return self.at(yh=1 - self.yh)
        if dim == "yl":
            return self.at(yl=1 - self.yl)
        if dim == "xa":
            return self.at(x=self.x + 1 - 2 * (self.x % 2))
        if dim == "xb":
            return self.at(x=(self.x + 3 + 2 * (self.x % 2)) % 4)
        if dim == "za":
            return self.at(z=self.z + 1 - 2 * (self.z % 2))
        return self.at(z=(self.z + 3 + 2 * (self.z % 2)) % 4)


ROW_ORDERS = (("xa", "xb", "yh"), ("xb", "yh", "xa"), ("yh", "xa", "xb"))
COL_ORDERS = (("za", "zb", "yl"), ("zb", "za", "yl"), ("za", "zb", "yl"), ("zb", "za", "yl"))


def greet(place, dims):
    barrier = pltpu.get_barrier_semaphore()
    for dim in dims:
        pl.semaphore_signal(barrier, inc=1, device_id=place.partner(dim), device_id_type=MESH)
    pl.semaphore_wait(barrier, len(dims))


def segments(place, base, length, dims):
    out = []
    start, n = base, length
    for dim in dims:
        n = n // 2
        bit = place.bits[dim]
        keep = pl.multiple_of(start + bit * n, 16)
        send = pl.multiple_of(start + (1 - bit) * n, 16)
        out.append((keep, send, n))
        start = keep
    return out


def block_of(n):
    for blk in (128, 112, 96, 80, 64, 48, 32, 16):
        if n % blk == 0:
            return blk
    return n


def add_rows(dst, dst_at, one, one_at, two, two_at, n):
    blk = block_of(n)

    def body(i, carry):
        o = i * blk
        a = one[pl.ds(pl.multiple_of(one_at + o, 16), blk), :].astype(F32)
        b = two[pl.ds(pl.multiple_of(two_at + o, 16), blk), :].astype(F32)
        dst[pl.ds(pl.multiple_of(dst_at + o, 16), blk), :] = (a + b).astype(dst.dtype)
        return carry

    lax.fori_loop(0, n // blk, body, 0)


def partial_kernel(rows_s, cols_s, count_s, omega_ref, series_ref, band_ref, row_ref, col_ref, racc_ref, cacc_ref):
    s = pl.program_id(0)
    count = count_s[0]

    def again(ids, t):
        seen = False
        for k in range(SLOTS - 1):
            seen = jnp.logical_or(seen, jnp.logical_and(k < t, ids[k] == ids[t]))
        return seen

    @pl.when(s < count)
    def _():
        half = omega_ref[0].astype(BF16)
        at = pl.multiple_of(cols_s[s] * TILE, TILE)
        panel = series_ref[:, pl.ds(at, TILE)]
        row_again = again(rows_s, s)
        col_again = again(cols_s, s)
        term = lax.dot_general(half, panel, (((1,), (1,)), ((), ())), preferred_element_type=F32)

        @pl.when(row_again)
        def _():
            racc_ref[rows_s[s]] += term

        @pl.when(jnp.logical_not(row_again))
        def _():
            racc_ref[rows_s[s]] = term

        term2 = jnp.dot(band_ref[0], half, preferred_element_type=F32)

        @pl.when(col_again)
        def _():
            cacc_ref[cols_s[s]] += term2

        @pl.when(jnp.logical_not(col_again))
        def _():
            cacc_ref[cols_s[s]] = term2

    @pl.when(s == SLOTS - 1)
    def _():
        def finish(ids, acc_ref, out_ref, blocks):
            def one(i, carry):
                held = False
                for k in range(SLOTS):
                    held = jnp.logical_or(held, jnp.logical_and(k < count, ids[k] == i))

                @pl.when(held)
                def _():
                    out_ref[i] = acc_ref[i].astype(BF16)

                @pl.when(jnp.logical_not(held))
                def _():
                    out_ref[i] = jnp.zeros(out_ref.shape[1:], BF16)

                return carry

            lax.fori_loop(0, blocks, one, 0)

        finish(rows_s, racc_ref, row_ref, BAND)
        finish(cols_s, cacc_ref, col_ref, BLK)


def band_kernel(series, band, sbuf, ss_b, rs_b, ss_y, ss_s, rs_s, ls):
    place = Place()
    core = place.core
    xs = place.yl * 2 + place.z // 2
    near = place.yh == place.z % 2
    source = jnp.logical_and(place.x == xs, near)
    sister = place.partner("core")
    over = place.partner("yh")
    dist = [(place.x - xs + 4) % 4, (xs - place.x + 4) % 4]
    onward = [place.at(x=(place.x + 1) % 4), place.at(x=(place.x + 3) % 4)]
    hops = [jnp.where(near, dist[s % 2], (dist[s % 2] + 4 - s // 2) % 4) for s in range(4)]
    lag = [jnp.where(near, 0, s // 2 + 1) + hops[s] for s in range(4)]
    crossing = [jnp.logical_and(near, dist[s % 2] == s // 2) for s in range(4)]

    def slot(i, which):
        return band.at[which * BLK + i // SPLIT, pl.ds(pl.multiple_of((i % SPLIT) * CH, 16), CH), :]

    def native(i):
        return sbuf.at[pl.ds(pl.multiple_of((i % SPLIT) * CH, 16), CH),
                       pl.ds(pl.multiple_of((i // SPLIT) * TILE, TILE), TILE)]

    def to_next(src, i, s):
        return pltpu.make_async_remote_copy(src, slot(i, core), ss_b.at[i], rs_b.at[i],
                                            device_id=onward[s % 2], device_id_type=MESH)

    def to_over(src, i):
        return pltpu.make_async_remote_copy(src, slot(i, core), ss_y.at[i], rs_b.at[i],
                                            device_id=over, device_id_type=MESH)

    def to_sister(src, i):
        return pltpu.make_async_remote_copy(src, slot(i, core), ss_s.at[i], rs_s.at[i],
                                            device_id=sister, device_id_type=MESH)

    def keep_native(i):
        return pltpu.make_async_copy(native(i), slot(i, core), ls.at[1 + i])

    load = pltpu.make_async_copy(series, sbuf, ls.at[0])

    @pl.when(source)
    def _():
        load.start()

    greet(place, ("core", "xa", "xb", "yh"))

    def forward(src, i, s):
        @pl.when(hops[s] < 3)
        def _():
            to_next(src, i, s).start()

        @pl.when(crossing[s])
        def _():
            to_over(src, i).start()

        to_sister(src, i).start()

    @pl.when(source)
    def _():
        load.wait()

        def emit(k, carry):
            for s in range(4):
                i = k * 4 + s
                forward(native(i), i, s)
                keep_native(i).start()
            return carry

        lax.fori_loop(0, CHUNKS // 4, emit, 0)

    @pl.when(jnp.logical_not(source))
    def _():
        def tick(t, carry):
            for s in range(4):
                k = t - lag[s]

                @pl.when(jnp.logical_and(k >= 0, k < CHUNKS // 4))
                def _():
                    i = k * 4 + s
                    to_next(slot(i, core), i, s).wait_recv()
                    forward(slot(i, core), i, s)

            return carry

        lax.fori_loop(0, CHUNKS // 4 + 5, tick, 0)

    def drain(k, carry):
        for s in range(4):
            i = k * 4 + s
            to_sister(slot(i, 1 - core), i).wait_recv()
            to_sister(slot(i, core), i).wait_send()

            @pl.when(hops[s] < 3)
            def _():
                to_next(slot(i, core), i, s).wait_send()

            @pl.when(crossing[s])
            def _():
                to_over(slot(i, core), i).wait_send()

            @pl.when(source)
            def _():
                keep_native(i).wait()

        return carry

    lax.fori_loop(0, CHUNKS // 4, drain, 0)


def sums_kernel(rowpart, colpart, rowhalf, colhalf, squares, racc, rcore, rrecv, rfin, cacc, crecv, cfin,
                ss_k, rs_k, ss_r, rs_r, ss_s, rs_s, ss_c, rs_c, ls):
    place = Place()
    core = place.core
    sister = place.partner("core")
    home = core * HALF
    away = (1 - core) * HALF

    rsegs = [segments(place, ROW_BASE[o], ROW_LEN[o], ROW_ORDERS[o]) for o in range(RCH)]
    csegs = [segments(place, COL_BASE[o], COL_LEN[o], COL_ORDERS[o]) for o in range(CCH)]

    def landing(segs):
        out, at = [], 0
        for line in segs:
            row = []
            for keep, send, n in line:
                row.append(at)
                at += n
            out.append(row)
        return out

    rland = landing(rsegs)
    cland = landing(csegs)

    def part_at(which, o):
        return rowpart.at[pl.ds(pl.multiple_of(which + ROW_BASE[o], 16), ROW_LEN[o])]

    def pair(o):
        at = pl.ds(ROW_BASE[o], ROW_LEN[o])
        return pltpu.make_async_remote_copy(part_at(away, o), rcore.at[at], ss_k.at[o], rs_k.at[o],
                                            device_id=sister, device_id_type=MESH)

    def row_load(o):
        at = pl.ds(ROW_BASE[o], ROW_LEN[o])
        return pltpu.make_async_copy(part_at(home, o), racc.at[at], ls.at[o])

    def col_load(o):
        keep, send, n = csegs[o][0]
        return pltpu.make_async_copy(colpart.at[pl.ds(keep, n)], cacc.at[pl.ds(keep, n)], ls.at[RCH + o])

    def row_send(o, j):
        keep, send, n = rsegs[o][j]
        return pltpu.make_async_remote_copy(
            racc.at[pl.ds(send, n)], rrecv.at[pl.ds(rland[o][j], n)], ss_r.at[o * 6 + j], rs_r.at[o * 6 + j],
            device_id=place.partner(ROW_ORDERS[o][j]), device_id_type=MESH)

    def col_send(o, j):
        keep, send, n = csegs[o][j]
        src = colpart if j == 0 else cacc
        return pltpu.make_async_remote_copy(
            src.at[pl.ds(send, n)], crecv.at[pl.ds(cland[o][j], n)], ss_c.at[o * 6 + j], rs_c.at[o * 6 + j],
            device_id=place.partner(COL_ORDERS[o][j]), device_id_type=MESH)

    def row_at(start, n):
        return rowhalf.at[pl.ds(pl.multiple_of(home + start, 16), n)]

    def row_gather(o, j):
        keep, send, n = rsegs[o][j]
        src = rfin.at[pl.ds(ROW_FIN[o], n)] if j == 2 else row_at(keep, n)
        return pltpu.make_async_remote_copy(
            src, row_at(keep, n), ss_r.at[o * 6 + 3 + j], rs_r.at[o * 6 + 3 + j],
            device_id=place.partner(ROW_ORDERS[o][j]), device_id_type=MESH)

    def row_local(o):
        keep, send, n = rsegs[o][2]
        return pltpu.make_async_copy(rfin.at[pl.ds(ROW_FIN[o], n)], row_at(keep, n), ls.at[RCH + CCH + o])

    def row_share(o, j):
        if j == 3:
            keep, send, n = rsegs[o][2]
            src, start = rfin.at[pl.ds(ROW_FIN[o], n)], keep
        else:
            keep, send, n = rsegs[o][j]
            src, start = row_at(send, n), send
        return pltpu.make_async_remote_copy(
            src, row_at(start, n), ss_s.at[o * 4 + j], rs_s.at[o * 4 + j], device_id=sister, device_id_type=MESH)

    def col_at(start, n):
        return colhalf.at[pl.ds(start, n)]

    def col_gather(o, j):
        keep, send, n = csegs[o][j]
        src = cfin.at[pl.ds(COL_FIN[o], n)] if j == 2 else col_at(keep, n)
        return pltpu.make_async_remote_copy(
            src, col_at(keep, n), ss_c.at[o * 6 + 3 + j], rs_c.at[o * 6 + 3 + j],
            device_id=place.partner(COL_ORDERS[o][j]), device_id_type=MESH)

    def col_local(o):
        keep, send, n = csegs[o][2]
        return pltpu.make_async_copy(cfin.at[pl.ds(COL_FIN[o], n)], col_at(keep, n), ls.at[2 * RCH + CCH + o])

    for o in range(RCH):
        row_load(o).start()
    for o in range(CCH):
        col_load(o).start()
    greet(place, ("core", "xa", "xb", "yh", "za", "zb", "yl"))
    for o in range(RCH):
        pair(o).start()
    for o in range(CCH):
        col_send(o, 0).start()
    for o in range(RCH):
        row_load(o).wait()
        pair(o).wait_recv()
        add_rows(racc, ROW_BASE[o], racc, ROW_BASE[o], rcore, ROW_BASE[o], ROW_LEN[o])
        row_send(o, 0).start()

    def col_add(o, j):
        keep, send, n = csegs[o][j]
        if j == 0:
            col_load(o).wait()
        col_send(o, j).wait_recv()
        if j < 2:
            add_rows(cacc, keep, cacc, keep, crecv, cland[o][j], n)
            col_send(o, j + 1).start()
        else:
            add_rows(cfin, COL_FIN[o], cacc, keep, crecv, cland[o][j], n)
            col_gather(o, 2).start()
            col_local(o).start()

    def row_add(o, j, total):
        keep, send, n = rsegs[o][j]
        row_send(o, j).wait_recv()
        if j < 2:
            add_rows(racc, keep, racc, keep, rrecv, rland[o][j], n)
            row_send(o, j + 1).start()
            return total

        def body(i, total):
            a = racc[pl.ds(pl.multiple_of(keep + i * 16, 16), 16), :].astype(F32)
            b = rrecv[pl.ds(pl.multiple_of(rland[o][2] + i * 16, 16), 16), :].astype(F32)
            c = a + b
            rfin[pl.ds(pl.multiple_of(ROW_FIN[o] + i * 16, 16), 16), :] = c.astype(BF16)
            c2 = c * c
            return total + c2[:8] + c2[8:]

        total = lax.fori_loop(0, n // 16, body, total)
        row_gather(o, 2).start()
        row_local(o).start()
        row_share(o, 3).start()
        return total

    total = jnp.zeros((8, SCANS), F32)
    for j in range(3):
        for o in range(max(RCH, CCH)):
            if o < CCH:
                col_add(o, j)
            if o < RCH:
                total = row_add(o, j, total)
    squares[...] = total

    def col_pass(o, j):
        if j == 2:
            col_local(o).wait()
        col_gather(o, j).wait_recv()
        if j > 0:
            col_gather(o, j - 1).start()

    def row_pass(o, j):
        if j == 2:
            row_local(o).wait()
        row_gather(o, j).wait_recv()
        if j > 0:
            row_gather(o, j - 1).start()
        row_share(o, j).start()

    for j in (2, 1, 0):
        for o in range(max(RCH, CCH)):
            if o < CCH:
                col_pass(o, j)
            if o < RCH:
                row_pass(o, j)
    for o in range(RCH):
        pair(o).wait_send()
        for j in range(4):
            row_share(o, j).wait_recv()
            row_share(o, j).wait_send()
        for j in range(3):
            row_send(o, j).wait_send()
            row_gather(o, j).wait_send()
    for o in range(CCH):
        for j in range(3):
            col_send(o, j).wait_send()
            col_gather(o, j).wait_send()


def update_kernel(rows_s, cols_s, count_s, omega_ref, rowhalf_ref, band_ref, series_ref, colhalf_ref,
                  out_ref, sums_ref, grad_ref, acc_ref, diag_ref):
    s = pl.program_id(0)
    live = s < count_s[0]
    row_base = lax.axis_index("row") * BAND
    col_base = lax.axis_index("col") * BLK

    @pl.when(s == 0)
    def _():
        acc_ref[...] = jnp.zeros_like(acc_ref)
        diag_ref[...] = jnp.zeros_like(diag_ref)

    @pl.when(jnp.logical_not(live))
    def _():
        out_ref[0] = jnp.zeros((TILE, TILE), F32)

    @pl.when(live)
    def _():
        grad_ref[...] = (0.5 / SCANS) * (
            jnp.dot(rowhalf_ref[0], series_ref[...], preferred_element_type=F32)
            + lax.dot_general(band_ref[0], colhalf_ref[0], (((0,), (0,)), ((), ())), preferred_element_type=F32)
        )
        blk = 32

        def fold(v):
            return v[0:8] + v[8:16] + v[16:24] + v[24:32]

        def body(i, carry):
            before, inner, moved, after = carry
            at = pl.ds(pl.multiple_of(i * blk, blk), blk)
            now = omega_ref[0, at, :]
            grad = grad_ref[at, :]
            stepped = now - STEP * grad
            updated = stepped - jnp.clip(stepped, -THRESH, THRESH)
            change = updated - now
            out_ref[0, at, :] = updated
            return (before + fold(jnp.abs(now)), inner + fold(grad * change), moved + fold(change * change),
                    after + fold(jnp.abs(updated)))

        zero = jnp.zeros((8, TILE), F32)
        before, inner, moved, after = lax.fori_loop(0, TILE // blk, body, (zero, zero, zero, zero))
        acc_ref[0] += before
        acc_ref[1] += inner
        acc_ref[2] += moved
        acc_ref[3] += after

        @pl.when(row_base + rows_s[s] == col_base + cols_s[s])
        def _():
            mask = lax.broadcasted_iota(jnp.int32, (128, 128), 0) == lax.broadcasted_iota(jnp.int32, (128, 128), 1)
            for q in range(TILE // 128):
                at = slice(q * 128, (q + 1) * 128)

                def pick(v):
                    return jnp.sum(jnp.where(mask, v, 0.0), axis=0, keepdims=True)

                now = pick(omega_ref[0, at, at])
                plain = pick(grad_ref[at, at])
                shrunk = out_ref[0, at, at]
                old = pick(shrunk)
                grad = plain - 1.0 / now
                stepped = now - STEP * grad
                change = stepped - now
                old_change = old - now
                out_ref[0, at, at] = jnp.where(mask, stepped, shrunk)
                diag_ref[0:1] += jnp.log(now)
                diag_ref[1:2] -= jnp.abs(now)
                diag_ref[2:3] += grad * change - plain * old_change
                diag_ref[3:4] += change * change - old_change * old_change
                diag_ref[4:5] -= jnp.abs(old)

    @pl.when(s == SLOTS - 1)
    def _():
        sums_ref[0:1] = diag_ref[0:1]
        for t in range(4):
            v = acc_ref[t]
            v = v[:, 0:128] + v[:, 128:256] + v[:, 256:384] + v[:, 384:512]
            sums_ref[1 + t:2 + t] = jnp.sum(v, axis=0, keepdims=True) + diag_ref[1 + t:2 + t]
        sums_ref[5:8] = jnp.zeros((3, 128), F32)


def total_kernel(sums, squares, out, vec, recv_a, recv_b, ss, rs):
    place = Place()
    row, col = place.row, place.col
    barrier = pltpu.get_barrier_semaphore()
    for k in range(1, 16):
        pl.semaphore_signal(barrier, inc=1, device_id=(row, (col + k) % 16), device_id_type=MESH)
    for k in range(1, 8):
        pl.semaphore_signal(barrier, inc=1, device_id=((row + k) % 8, col), device_id_type=MESH)
    v = squares[...]
    v = jnp.sum(v, axis=0, keepdims=True)
    v = v[:, 0:128] + v[:, 128:256] + v[:, 256:384]
    spot = lax.broadcasted_iota(jnp.int32, (8, 128), 0) == 5
    vec[0] = sums[...] + jnp.where(spot, jnp.broadcast_to(v, (8, 128)), 0.0)
    pl.semaphore_wait(barrier, 22)

    def across(k):
        return pltpu.make_async_remote_copy(vec.at[0], recv_a.at[col], ss.at[k - 1], rs.at[k - 1],
                                            device_id=(row, (col + k) % 16), device_id_type=MESH)

    def down(k):
        return pltpu.make_async_remote_copy(vec.at[1], recv_b.at[row], ss.at[14 + k], rs.at[14 + k],
                                            device_id=((row + k) % 8, col), device_id_type=MESH)

    for k in range(1, 16):
        across(k).start()
    recv_a[col] = vec[0]
    for k in range(1, 16):
        across(k).wait_recv()
    total = recv_a[0]
    for k in range(1, 16):
        total = total + recv_a[k]
    vec[1] = total
    for k in range(1, 8):
        down(k).start()
    recv_b[row] = total
    for k in range(1, 8):
        down(k).wait_recv()
    total = recv_b[0]
    for k in range(1, 8):
        total = total + recv_b[k]
    s = jnp.sum(total, axis=1, keepdims=True)
    smooth = -s[0:1] + s[5:6] / (2.0 * SCANS)
    objective = smooth + PENALTY * s[1:2]
    bound = smooth + s[2:3] + s[3:4] / (2.0 * STEP) + PENALTY * s[4:5]
    out[0] = objective[0, 0]
    out[1] = bound[0, 0]
    for k in range(1, 16):
        across(k).wait_send()
    for k in range(1, 8):
        down(k).wait_send()


def plain(**kw):
    return pltpu.CompilerParams(vmem_limit_bytes=60 << 20, **kw)


dma = pltpu.SemaphoreType.DMA
VMEM = pl.BlockSpec(memory_space=pltpu.VMEM)
HBM = pl.BlockSpec(memory_space=pl.ANY)


def band_call(series, cid):
    return pl.pallas_call(
        band_kernel,
        out_shape=jax.ShapeDtypeStruct((BAND, SCANS, TILE), BF16),
        in_specs=[HBM], out_specs=HBM,
        scratch_shapes=[pltpu.VMEM((SCANS, BLK * TILE), BF16),
                        dma((CHUNKS,)), dma((CHUNKS,)), dma((CHUNKS,)), dma((CHUNKS,)), dma((CHUNKS,)),
                        dma((CHUNKS + 1,))],
        compiler_params=plain(collective_id=cid, has_side_effects=True), name="band",
    )(series)


def sums_call(row_part, col_part, cid):
    return pl.pallas_call(
        sums_kernel,
        out_shape=(jax.ShapeDtypeStruct((ROWS, SCANS), BF16), jax.ShapeDtypeStruct((COLS, TILE), BF16),
                   jax.ShapeDtypeStruct((8, SCANS), F32)),
        in_specs=[HBM, HBM], out_specs=(HBM, HBM, VMEM),
        scratch_shapes=[pltpu.VMEM((HALF, SCANS), BF16), pltpu.VMEM((HALF, SCANS), BF16),
                        pltpu.VMEM((HALF * 7 // 8, SCANS), BF16), pltpu.VMEM((HALF // 8, SCANS), BF16),
                        pltpu.VMEM((COLS, TILE), BF16), pltpu.VMEM((COLS * 7 // 8, TILE), BF16),
                        pltpu.VMEM((COLS // 8, TILE), BF16),
                        dma((RCH,)), dma((RCH,)), dma((6 * RCH,)), dma((6 * RCH,)),
                        dma((4 * RCH,)), dma((4 * RCH,)), dma((6 * CCH,)), dma((6 * CCH,)),
                        dma((2 * RCH + 2 * CCH,))],
        compiler_params=plain(collective_id=cid, has_side_effects=True), name="sums",
    )(row_part, col_part)


def local(series, omega_tiles, tile_row, tile_col, tile_count):
    omega = omega_tiles[0, 0]
    rows_s = tile_row[0, 0]
    cols_s = tile_col[0, 0]
    count = tile_count[0]
    band = band_call(series, 0)
    row_part, col_part = pl.pallas_call(
        partial_kernel,
        out_shape=(jax.ShapeDtypeStruct((BAND, TILE, SCANS), BF16), jax.ShapeDtypeStruct((BLK, SCANS, TILE), BF16)),
        grid_spec=pltpu.PrefetchScalarGridSpec(
            num_scalar_prefetch=3, grid=(SLOTS,),
            in_specs=[pl.BlockSpec((1, TILE, TILE), lambda s, *_: (s, 0, 0)),
                      pl.BlockSpec((SCANS, BLK * TILE), lambda s, *_: (0, 0)),
                      pl.BlockSpec((1, SCANS, TILE), lambda s, r, c, m: (r[s], 0, 0))],
            out_specs=(pl.BlockSpec((BAND, TILE, SCANS), lambda s, *_: (0, 0, 0)),
                       pl.BlockSpec((BLK, SCANS, TILE), lambda s, *_: (0, 0, 0))),
            scratch_shapes=[pltpu.VMEM((BAND, TILE, SCANS), F32), pltpu.VMEM((BLK, SCANS, TILE), F32)]),
        compiler_params=plain(), name="partials",
    )(rows_s, cols_s, count, omega, series, band)

    row_half, col_half, squares = sums_call(row_part.reshape(ROWS, SCANS), col_part.reshape(COLS, TILE), 1)
    omega_next, sums = pl.pallas_call(
        update_kernel,
        out_shape=(jax.ShapeDtypeStruct((SLOTS, TILE, TILE), F32), jax.ShapeDtypeStruct((8, 128), F32)),
        grid_spec=pltpu.PrefetchScalarGridSpec(
            num_scalar_prefetch=3, grid=(SLOTS,),
            in_specs=[pl.BlockSpec((1, TILE, TILE), lambda s, *_: (s, 0, 0)),
                      pl.BlockSpec((1, TILE, SCANS), lambda s, r, c, m: (r[s], 0, 0)),
                      pl.BlockSpec((1, SCANS, TILE), lambda s, r, c, m: (r[s], 0, 0)),
                      pl.BlockSpec((SCANS, TILE), lambda s, r, c, m: (0, c[s])),
                      pl.BlockSpec((1, SCANS, TILE), lambda s, r, c, m: (c[s], 0, 0))],
            out_specs=(pl.BlockSpec((1, TILE, TILE), lambda s, *_: (s, 0, 0)),
                       pl.BlockSpec((8, 128), lambda s, *_: (0, 0))),
            scratch_shapes=[pltpu.VMEM((TILE, TILE), F32), pltpu.VMEM((4, 8, TILE), F32), pltpu.VMEM((8, 128), F32)]),
        compiler_params=plain(), name="update",
    )(rows_s, cols_s, count, omega, row_half.reshape(BAND, TILE, SCANS), band, series, col_half.reshape(BLK, SCANS, TILE))

    values = pl.pallas_call(
        total_kernel,
        out_shape=jax.ShapeDtypeStruct((2,), F32),
        in_specs=[VMEM, VMEM], out_specs=pl.BlockSpec(memory_space=pltpu.SMEM),
        scratch_shapes=[pltpu.VMEM((2, 8, 128), F32), pltpu.VMEM((16, 8, 128), F32), pltpu.VMEM((8, 8, 128), F32),
                        pltpu.SemaphoreType.DMA((22,)), pltpu.SemaphoreType.DMA((22,))],
        compiler_params=plain(collective_id=2, has_side_effects=True), name="total",
    )(sums, squares)
    return omega_next[None, None], values


def solution(mesh):
    placed = (
        P(None, "col"),
        P("row", "col", None, None, None),
        P("row", "col", None),
        P("row", "col", None),
        P("row", "col"),
    )
    return jax.shard_map(
        local,
        mesh=mesh,
        in_specs=placed,
        out_specs=(P("row", "col", None, None, None), P()),
        check_vma=False,
    )
```

time: 229 us -> 182 us (0.79)
  Pallas kernels: 226 us -> 179 us
    pallas_call x5 -> x4, Pallas kernels: 206 us -> 159 us  [the longest x1 91.6 us: sums_call(): pl.pallas_call(sums_kernel, out_shape=(jax.ShapeDtypeStruct((ROWS, SCANS)...]
where the time goes in v2:
time: 182 us; the launch traced here: 181 us
  Pallas kernels  179 us (98%)
    pallas_call x1, Pallas kernels, sums_call(): pl.pallas_call(sums_kernel, out_shape=(jax.ShapeDtypeStruct((ROWS, SCANS)...  91.6 us
    pallas_call x1, Pallas kernels, band_call(): pl.pallas_call(band_kernel, out_shape=jax.ShapeDtypeStruct((BAND, SCANS,...  34.3 us
    pallas_call x1, Pallas kernels, local(): pl.pallas_call(update_kernel, out_shape=(jax.ShapeDtypeStruct((SLOTS, TIL...  20.2 us
    pallas_call x1, Pallas kernels, local(): pl.pallas_call(partial_kernel, out_shape=(jax.ShapeDtypeStruct((BAND, TIL...  19.2 us
    pallas_call x1, Pallas kernels, local(): pl.pallas_call(total_kernel, out_shape=jax.ShapeDtypeStruct((2,), F32), i...  13.6 us

profile of v2, /device:TPU:1, one launch (start us, length us, event | category | flops | bytes accessed | tf_op | source)
XLA Modules:
  0.0 181.3 jit_solution(6105431170051218982)
XLA Ops:
  1.3 34.3 %band.1.band_ref = bf16[14,384,512]{2,1,0:T(8,128)(2,1)} custom-call(bf16[384,3584]{1,0:T(8,128)(2,1)} %series_ref.3), custom_call_target="tpu_custom_call" | custom-call | tf_op jit(solution)/shard_map/band/pallas_call | solution.py:632
  35.6 19.2 %partials.1 = (bf16[14,512,384]{2,1,0:T(8,128)(2,1)}, bf16[7,384,512]{2,1,0:T(8,128)(2,1)}) custom-call(s32[10]{0:T(128)} %bitcast.17, s32[10]{0:T(128)} %bitcast.19, s32[1]{0:T(128)} %bitcast.9.count_s, f32[10,512,512]{2,1,0:T(8,128)} %bitcast.11, bf16[384,3584]{1,0:T(8,128)(2,1)} %series_ref.3, bf16[14,384,512]{2,1,0:T(8,128)(2,1)} %band.1.band_ref), custom_call_target="tpu_custom_call" | custom-call | tf_op jit(solution)/shard_map/partials/pallas_call | solution.py:666
  54.8 91.6 %sums.1 = (bf16[7168,384]{1,0:T(8,128)(2,1)}, bf16[2688,512]{1,0:T(8,128)(2,1)}, f32[8,384]{1,0:T(8,128)}) custom-call(bf16[7168,384]{1,0:T(8,128)(2,1)} %bitcast.14, bf16[2688,512]{1,0:T(8,128)(2,1)} %bitcast.16), custom_call_target="tpu_custom_call" | custom-call | tf_op jit(solution)/shard_map/sums/pallas_call | solution.py:644
  146.4 20.2 %update.1 = (f32[10,512,512]{2,1,0:T(8,128)}, f32[8,128]{1,0:T(8,128)}) custom-call(s32[10]{0:T(128)} %bitcast.18, s32[10]{0:T(128)} %bitcast.20, s32[1]{0:T(128)} %bitcast.10.count_s, f32[10,512,512]{2,1,0:T(8,128)} %bitcast.12, bf16[14,512,384]{2,1,0:T(8,128)(2,1)} %bitcast.13, bf16[14,384,512]{2,1,0:T(8,128)(2,1)} %band.1.band_ref, ...), custom_call_target="tpu_custom_call" | custom-call | tf_op jit(solution)/shard_map/update/pallas_call | solution.py:681
  166.6 13.6 %total.1 = f32[2]{0:T(128)} custom-call(f32[8,128]{1,0:T(8,128)} %get-tuple-element.14.sums, f32[8,384]{1,0:T(8,128)} %get-tuple-element.15.squares), custom_call_target="tpu_custom_call" | custom-call | tf_op jit(solution)/shard_map/total/pallas_call | solution.py:697
  180.2 1.1 copy.9

commit v3 on v2

--- a/solution.py
+++ b/solution.py
@@ -25,7 +25,7 @@
 HALF = ROWS // 2
 ROW_LEN = (1152, 1152, 1280)
 COLS = BLK * SCANS
-COL_LEN = (640, 640, 640, 768)
+COL_LEN = (512, 512, 384, 512, 384, 384)
 SPLIT = 4
 CHUNKS = BLK * SPLIT
 CH = SCANS // SPLIT
@@ -91,7 +91,7 @@
 
 
 ROW_ORDERS = (("xa", "xb", "yh"), ("xb", "yh", "xa"), ("yh", "xa", "xb"))
-COL_ORDERS = (("za", "zb", "yl"), ("zb", "za", "yl"), ("za", "zb", "yl"), ("zb", "za", "yl"))
+COL_ORDERS = (("za", "zb", "yl"), ("zb", "za", "yl")) * 3
 
 
 def greet(place, dims):
@@ -134,23 +134,62 @@
     lax.fori_loop(0, n // blk, body, 0)
 
 
-def partial_kernel(rows_s, cols_s, count_s, omega_ref, series_ref, band_ref, row_ref, col_ref, racc_ref, cacc_ref):
-    s = pl.program_id(0)
+def partial_kernel(rows_s, cols_s, count_s, omega_h, series_h, band_h, row_ref, col_ref, omega_ref, series_ref, band_ref,
+                   racc_ref, cacc_ref, rout_ref, cout_ref, isem, rsem, csem):
     count = count_s[0]
 
+    def loads(s):
+        at = pl.multiple_of(cols_s[s] * TILE, TILE)
+        return (pltpu.make_async_copy(omega_h.at[s], omega_ref.at[s], isem.at[s, 0]),
+                pltpu.make_async_copy(series_h.at[:, pl.ds(at, TILE)], series_ref.at[s], isem.at[s, 1]),
+                pltpu.make_async_copy(band_h.at[rows_s[s]], band_ref.at[s], isem.at[s, 2]))
+
+    def fetch(s, carry):
+        for load in loads(s):
+            load.start()
+        return carry
+
+    lax.fori_loop(0, count, fetch, 0)
+
+    def row_out(i):
+        return pltpu.make_async_copy(rout_ref.at[i], row_ref.at[i], rsem.at[i])
+
+    def col_out(i):
+        return pltpu.make_async_copy(cout_ref.at[i], col_ref.at[i], csem.at[i])
+
+    def clear(ids, stage, out, blocks):
+        def one(i, carry):
+            held = False
+            for k in range(SLOTS):
+                held = jnp.logical_or(held, jnp.logical_and(k < count, ids[k] == i))
+
+            @pl.when(jnp.logical_not(held))
+            def _():
+                stage[i] = jnp.zeros(stage.shape[1:], BF16)
+                out(i).start()
+
+            return carry
+
+        lax.fori_loop(0, blocks, one, 0)
+
+    clear(rows_s, rout_ref, row_out, BAND)
+    clear(cols_s, cout_ref, col_out, BLK)
+
     def again(ids, t):
-        seen = False
-        for k in range(SLOTS - 1):
-            seen = jnp.logical_or(seen, jnp.logical_and(k < t, ids[k] == ids[t]))
-        return seen
-
-    @pl.when(s < count)
-    def _():
-        half = omega_ref[0].astype(BF16)
-        at = pl.multiple_of(cols_s[s] * TILE, TILE)
-        panel = series_ref[:, pl.ds(at, TILE)]
-        row_again = again(rows_s, s)
-        col_again = again(cols_s, s)
+        seen, more = False, False
+        for k in range(SLOTS):
+            same = ids[k] == ids[t]
+            seen = jnp.logical_or(seen, jnp.logical_and(k < t, same))
+            more = jnp.logical_or(more, jnp.logical_and(jnp.logical_and(k > t, k < count), same))
+        return seen, jnp.logical_not(more)
+
+    def work(s, carry):
+        for load in loads(s):
+            load.wait()
+        half = omega_ref[s].astype(BF16)
+        panel = series_ref[s]
+        row_again, row_last = again(rows_s, s)
+        col_again, col_last = again(cols_s, s)
         term = lax.dot_general(half, panel, (((1,), (1,)), ((), ())), preferred_element_type=F32)
 
         @pl.when(row_again)
@@ -161,7 +200,7 @@
         def _():
             racc_ref[rows_s[s]] = term
 
-        term2 = jnp.dot(band_ref[0], half, preferred_element_type=F32)
+        term2 = jnp.dot(band_ref[s], half, preferred_element_type=F32)
 
         @pl.when(col_again)
         def _():
@@ -171,28 +210,23 @@
         def _():
             cacc_ref[cols_s[s]] = term2
 
-    @pl.when(s == SLOTS - 1)
-    def _():
-        def finish(ids, acc_ref, out_ref, blocks):
-            def one(i, carry):
-                held = False
-                for k in range(SLOTS):
-                    held = jnp.logical_or(held, jnp.logical_and(k < count, ids[k] == i))
-
-                @pl.when(held)
-                def _():
-                    out_ref[i] = acc_ref[i].astype(BF16)
-
-                @pl.when(jnp.logical_not(held))
-                def _():
-                    out_ref[i] = jnp.zeros(out_ref.shape[1:], BF16)
-
-                return carry
-
-            lax.fori_loop(0, blocks, one, 0)
-
-        finish(rows_s, racc_ref, row_ref, BAND)
-        finish(cols_s, cacc_ref, col_ref, BLK)
+        @pl.when(row_last)
+        def _():
+            rout_ref[rows_s[s]] = racc_ref[rows_s[s]].astype(BF16)
+            row_out(rows_s[s]).start()
+
+        @pl.when(col_last)
+        def _():
+            cout_ref[cols_s[s]] = cacc_ref[cols_s[s]].astype(BF16)
+            col_out(cols_s[s]).start()
+
+        return carry
+
+    lax.fori_loop(0, count, work, 0)
+    for i in range(BAND):
+        row_out(i).wait()
+    for i in range(BLK):
+        col_out(i).wait()
 
 
 def band_kernel(series, band, sbuf, ss_b, rs_b, ss_y, ss_s, rs_s, ls):
@@ -212,8 +246,8 @@
     def slot(i, which):
         return band.at[which * BLK + i // SPLIT, pl.ds(pl.multiple_of((i % SPLIT) * CH, 16), CH), :]
 
-    def native(i):
-        return sbuf.at[pl.ds(pl.multiple_of((i % SPLIT) * CH, 16), CH),
+    def native(i, held):
+        return held.at[pl.ds(pl.multiple_of((i % SPLIT) * CH, 16), CH),
                        pl.ds(pl.multiple_of((i // SPLIT) * TILE, TILE), TILE)]
 
     def to_next(src, i, s):
@@ -229,7 +263,7 @@
                                             device_id=sister, device_id_type=MESH)
 
     def keep_native(i):
-        return pltpu.make_async_copy(native(i), slot(i, core), ls.at[1 + i])
+        return pltpu.make_async_copy(native(i, sbuf), slot(i, core), ls.at[1 + i])
 
     load = pltpu.make_async_copy(series, sbuf, ls.at[0])
 
@@ -252,16 +286,20 @@
 
     @pl.when(source)
     def _():
-        load.wait()
-
         def emit(k, carry):
             for s in range(4):
                 i = k * 4 + s
-                forward(native(i), i, s)
-                keep_native(i).start()
+                forward(native(i, series), i, s)
             return carry
 
         lax.fori_loop(0, CHUNKS // 4, emit, 0)
+        load.wait()
+
+        def hold(i, carry):
+            keep_native(i).start()
+            return carry
+
+        lax.fori_loop(0, CHUNKS, hold, 0)
 
     @pl.when(jnp.logical_not(source))
     def _():
@@ -487,51 +525,72 @@
             col_gather(o, j).wait_send()
 
 
-def update_kernel(rows_s, cols_s, count_s, omega_ref, rowhalf_ref, band_ref, series_ref, colhalf_ref,
-                  out_ref, sums_ref, grad_ref, acc_ref, diag_ref):
-    s = pl.program_id(0)
-    live = s < count_s[0]
+def update_kernel(rows_s, cols_s, count_s, omega_h, rowhalf_h, band_h, series_h, colhalf_h, out_h, sums_ref,
+                  omega_ref, rowhalf_ref, band_ref, series_ref, colhalf_ref, out_ref, zero_ref,
+                  grad_ref, acc_ref, diag_ref, isem, osem):
+    count = count_s[0]
     row_base = lax.axis_index("row") * BAND
     col_base = lax.axis_index("col") * BLK
 
-    @pl.when(s == 0)
-    def _():
-        acc_ref[...] = jnp.zeros_like(acc_ref)
-        diag_ref[...] = jnp.zeros_like(diag_ref)
-
-    @pl.when(jnp.logical_not(live))
-    def _():
-        out_ref[0] = jnp.zeros((TILE, TILE), F32)
-
-    @pl.when(live)
-    def _():
-        grad_ref[...] = (0.5 / SCANS) * (
-            jnp.dot(rowhalf_ref[0], series_ref[...], preferred_element_type=F32)
-            + lax.dot_general(band_ref[0], colhalf_ref[0], (((0,), (0,)), ((), ())), preferred_element_type=F32)
-        )
-        blk = 32
+    def loads(s):
+        at = pl.multiple_of(cols_s[s] * TILE, TILE)
+        return (pltpu.make_async_copy(omega_h.at[s], omega_ref.at[s], isem.at[s, 0]),
+                pltpu.make_async_copy(rowhalf_h.at[rows_s[s]], rowhalf_ref.at[s], isem.at[s, 1]),
+                pltpu.make_async_copy(band_h.at[rows_s[s]], band_ref.at[s], isem.at[s, 2]),
+                pltpu.make_async_copy(series_h.at[:, pl.ds(at, TILE)], series_ref.at[s], isem.at[s, 3]),
+                pltpu.make_async_copy(colhalf_h.at[cols_s[s]], colhalf_ref.at[s], isem.at[s, 4]))
+
+    def store(s):
+        return pltpu.make_async_copy(out_ref.at[s], out_h.at[s], osem.at[s])
+
+    def store_zero(s):
+        return pltpu.make_async_copy(zero_ref, out_h.at[s], osem.at[s])
+
+    def fetch(s, carry):
+        for load in loads(s):
+            load.start()
+        return carry
+
+    lax.fori_loop(0, count, fetch, 0)
+    zero_ref[...] = jnp.zeros_like(zero_ref)
+    acc_ref[...] = jnp.zeros_like(acc_ref)
+    diag_ref[...] = jnp.zeros_like(diag_ref)
+
+    def clear(s, carry):
+        store_zero(s).start()
+        return carry
+
+    lax.fori_loop(count, SLOTS, clear, 0)
+
+    def work(s, carry):
+        for load in loads(s):
+            load.wait()
+        panel = series_ref[s]
+        sums = colhalf_ref[s]
+        blk = 128
 
         def fold(v):
-            return v[0:8] + v[8:16] + v[16:24] + v[24:32]
-
-        def body(i, carry):
-            before, inner, moved, after = carry
-            at = pl.ds(pl.multiple_of(i * blk, blk), blk)
-            now = omega_ref[0, at, :]
-            grad = grad_ref[at, :]
+            return jnp.sum(v.reshape(blk // 8, 8, TILE), axis=0)
+
+        before, model, after = acc_ref[0], acc_ref[1], acc_ref[2]
+        for i in range(TILE // blk):
+            at = slice(i * blk, (i + 1) * blk)
+            grad = (0.5 / SCANS) * (
+                jnp.dot(rowhalf_ref[s, at, :], panel, preferred_element_type=F32)
+                + lax.dot_general(band_ref[s, :, at], sums, (((0,), (0,)), ((), ())), preferred_element_type=F32)
+            )
+            now = omega_ref[s, at, :]
+            grad_ref[at, :] = grad
             stepped = now - STEP * grad
             updated = stepped - jnp.clip(stepped, -THRESH, THRESH)
             change = updated - now
-            out_ref[0, at, :] = updated
-            return (before + fold(jnp.abs(now)), inner + fold(grad * change), moved + fold(change * change),
-                    after + fold(jnp.abs(updated)))
-
-        zero = jnp.zeros((8, TILE), F32)
-        before, inner, moved, after = lax.fori_loop(0, TILE // blk, body, (zero, zero, zero, zero))
-        acc_ref[0] += before
-        acc_ref[1] += inner
-        acc_ref[2] += moved
-        acc_ref[3] += after
+            out_ref[s, at, :] = updated
+            before += fold(jnp.abs(now))
+            model += fold(change * (grad + change * (0.5 / STEP)))
+            after += fold(jnp.abs(updated))
+        acc_ref[0] = before
+        acc_ref[1] = model
+        acc_ref[2] = after
 
         @pl.when(row_base + rows_s[s] == col_base + cols_s[s])
         def _():
@@ -542,29 +601,42 @@
                 def pick(v):
                     return jnp.sum(jnp.where(mask, v, 0.0), axis=0, keepdims=True)
 
-                now = pick(omega_ref[0, at, at])
+                now = pick(omega_ref[s, at, at])
                 plain = pick(grad_ref[at, at])
-                shrunk = out_ref[0, at, at]
+                shrunk = out_ref[s, at, at]
                 old = pick(shrunk)
                 grad = plain - 1.0 / now
                 stepped = now - STEP * grad
                 change = stepped - now
                 old_change = old - now
-                out_ref[0, at, at] = jnp.where(mask, stepped, shrunk)
+                out_ref[s, at, at] = jnp.where(mask, stepped, shrunk)
                 diag_ref[0:1] += jnp.log(now)
                 diag_ref[1:2] -= jnp.abs(now)
-                diag_ref[2:3] += grad * change - plain * old_change
-                diag_ref[3:4] += change * change - old_change * old_change
-                diag_ref[4:5] -= jnp.abs(old)
-
-    @pl.when(s == SLOTS - 1)
-    def _():
-        sums_ref[0:1] = diag_ref[0:1]
-        for t in range(4):
-            v = acc_ref[t]
-            v = v[:, 0:128] + v[:, 128:256] + v[:, 256:384] + v[:, 384:512]
-            sums_ref[1 + t:2 + t] = jnp.sum(v, axis=0, keepdims=True) + diag_ref[1 + t:2 + t]
-        sums_ref[5:8] = jnp.zeros((3, 128), F32)
+                diag_ref[2:3] += (change * (grad + change * (0.5 / STEP))
+                                  - old_change * (plain + old_change * (0.5 / STEP)))
+                diag_ref[3:4] -= jnp.abs(old)
+
+        store(s).start()
+        return carry
+
+    lax.fori_loop(0, count, work, 0)
+    sums_ref[0:1] = diag_ref[0:1]
+    for t in range(3):
+        v = acc_ref[t]
+        v = v[:, 0:128] + v[:, 128:256] + v[:, 256:384] + v[:, 384:512]
+        sums_ref[1 + t:2 + t] = jnp.sum(v, axis=0, keepdims=True) + diag_ref[1 + t:2 + t]
+    sums_ref[4:8] = jnp.zeros((4, 128), F32)
+
+    def done(s, carry):
+        store(s).wait()
+        return carry
+
+    def cleared(s, carry):
+        store_zero(s).wait()
+        return carry
+
+    lax.fori_loop(0, count, done, 0)
+    lax.fori_loop(count, SLOTS, cleared, 0)
 
 
 def total_kernel(sums, squares, out, vec, recv_a, recv_b, ss, rs):
@@ -610,7 +682,7 @@
     s = jnp.sum(total, axis=1, keepdims=True)
     smooth = -s[0:1] + s[5:6] / (2.0 * SCANS)
     objective = smooth + PENALTY * s[1:2]
-    bound = smooth + s[2:3] + s[3:4] / (2.0 * STEP) + PENALTY * s[4:5]
+    bound = smooth + s[2:3] + PENALTY * s[3:4]
     out[0] = objective[0, 0]
     out[1] = bound[0, 0]
     for k in range(1, 16):
@@ -657,43 +729,50 @@
     )(row_part, col_part)
 
 
+def partials_call(rows_s, cols_s, count, omega, series, band):
+    return pl.pallas_call(
+        partial_kernel,
+        out_shape=(jax.ShapeDtypeStruct((BAND, TILE, SCANS), BF16), jax.ShapeDtypeStruct((BLK, SCANS, TILE), BF16)),
+        grid_spec=pltpu.PrefetchScalarGridSpec(
+            num_scalar_prefetch=3, grid=(),
+            in_specs=[HBM, HBM, HBM],
+            out_specs=(HBM, HBM),
+            scratch_shapes=[pltpu.VMEM((SLOTS, TILE, TILE), F32), pltpu.VMEM((SLOTS, SCANS, TILE), BF16),
+                            pltpu.VMEM((SLOTS, SCANS, TILE), BF16),
+                            pltpu.VMEM((BAND, TILE, SCANS), F32), pltpu.VMEM((BLK, SCANS, TILE), F32),
+                            pltpu.VMEM((BAND, TILE, SCANS), BF16), pltpu.VMEM((BLK, SCANS, TILE), BF16),
+                            dma((SLOTS, 3)), dma((BAND,)), dma((BLK,))]),
+        compiler_params=plain(), name="partials",
+    )(rows_s, cols_s, count, omega, series, band)
+
+
+def update_call(rows_s, cols_s, count, omega, row_half, band, series, col_half):
+    return pl.pallas_call(
+        update_kernel,
+        out_shape=(jax.ShapeDtypeStruct((SLOTS, TILE, TILE), F32), jax.ShapeDtypeStruct((8, 128), F32)),
+        grid_spec=pltpu.PrefetchScalarGridSpec(
+            num_scalar_prefetch=3, grid=(),
+            in_specs=[HBM, HBM, HBM, HBM, HBM],
+            out_specs=(HBM, VMEM),
+            scratch_shapes=[pltpu.VMEM((SLOTS, TILE, TILE), F32), pltpu.VMEM((SLOTS, TILE, SCANS), BF16),
+                            pltpu.VMEM((SLOTS, SCANS, TILE), BF16), pltpu.VMEM((SLOTS, SCANS, TILE), BF16),
+                            pltpu.VMEM((SLOTS, SCANS, TILE), BF16), pltpu.VMEM((SLOTS, TILE, TILE), F32),
+                            pltpu.VMEM((TILE, TILE), F32),
+                            pltpu.VMEM((TILE, TILE), F32), pltpu.VMEM((3, 8, TILE), F32), pltpu.VMEM((8, 128), F32),
+                            dma((SLOTS, 5)), dma((SLOTS,))]),
+        compiler_params=plain(), name="update",
+    )(rows_s, cols_s, count, omega, row_half.reshape(BAND, TILE, SCANS), band, series, col_half.reshape(BLK, SCANS, TILE))
+
+
 def local(series, omega_tiles, tile_row, tile_col, tile_count):
     omega = omega_tiles[0, 0]
     rows_s = tile_row[0, 0]
     cols_s = tile_col[0, 0]
     count = tile_count[0]
     band = band_call(series, 0)
-    row_part, col_part = pl.pallas_call(
-        partial_kernel,
-        out_shape=(jax.ShapeDtypeStruct((BAND, TILE, SCANS), BF16), jax.ShapeDtypeStruct((BLK, SCANS, TILE), BF16)),
-        grid_spec=pltpu.PrefetchScalarGridSpec(
-            num_scalar_prefetch=3, grid=(SLOTS,),
-            in_specs=[pl.BlockSpec((1, TILE, TILE), lambda s, *_: (s, 0, 0)),
-                      pl.BlockSpec((SCANS, BLK * TILE), lambda s, *_: (0, 0)),
-                      pl.BlockSpec((1, SCANS, TILE), lambda s, r, c, m: (r[s], 0, 0))],
-            out_specs=(pl.BlockSpec((BAND, TILE, SCANS), lambda s, *_: (0, 0, 0)),
-                       pl.BlockSpec((BLK, SCANS, TILE), lambda s, *_: (0, 0, 0))),
-            scratch_shapes=[pltpu.VMEM((BAND, TILE, SCANS), F32), pltpu.VMEM((BLK, SCANS, TILE), F32)]),
-        compiler_params=plain(), name="partials",
-    )(rows_s, cols_s, count, omega, series, band)
-
+    row_part, col_part = partials_call(rows_s, cols_s, count, omega, series, band)
     row_half, col_half, squares = sums_call(row_part.reshape(ROWS, SCANS), col_part.reshape(COLS, TILE), 1)
-    omega_next, sums = pl.pallas_call(
-        update_kernel,
-        out_shape=(jax.ShapeDtypeStruct((SLOTS, TILE, TILE), F32), jax.ShapeDtypeStruct((8, 128), F32)),
-        grid_spec=pltpu.PrefetchScalarGridSpec(
-            num_scalar_prefetch=3, grid=(SLOTS,),
-            in_specs=[pl.BlockSpec((1, TILE, TILE), lambda s, *_: (s, 0, 0)),
-                      pl.BlockSpec((1, TILE, SCANS), lambda s, r, c, m: (r[s], 0, 0)),
-                      pl.BlockSpec((1, SCANS, TILE), lambda s, r, c, m: (r[s], 0, 0)),
-                      pl.BlockSpec((SCANS, TILE), lambda s, r, c, m: (0, c[s])),
-                      pl.BlockSpec((1, SCANS, TILE), lambda s, r, c, m: (c[s], 0, 0))],
-            out_specs=(pl.BlockSpec((1, TILE, TILE), lambda s, *_: (s, 0, 0)),
-                       pl.BlockSpec((8, 128), lambda s, *_: (0, 0))),
-            scratch_shapes=[pltpu.VMEM((TILE, TILE), F32), pltpu.VMEM((4, 8, TILE), F32), pltpu.VMEM((8, 128), F32)]),
-        compiler_params=plain(), name="update",
-    )(rows_s, cols_s, count, omega, row_half.reshape(BAND, TILE, SCANS), band, series, col_half.reshape(BLK, SCANS, TILE))
-
+    omega_next, sums = update_call(rows_s, cols_s, count, omega, row_half, band, series, col_half)
     values = pl.pallas_call(
         total_kernel,
         out_shape=jax.ShapeDtypeStruct((2,), F32),

time: 182 us -> 172 us (0.945); the launches traced: 181 us -> 169 us
  Pallas kernels: 179 us -> 167 us
    pallas_call x2, Pallas kernels: 39.4 us -> 28.3 us  [the longest x1 14.5 us: update_call(): pl.pallas_call(update_kernel, out_shape=(jax.ShapeDtypeStruct((SLOTS, TIL...]
where the time goes in v3:
time: 172 us; the launch traced here: 169 us
  Pallas kernels  167 us (97%)
    pallas_call x1, Pallas kernels, sums_call(): pl.pallas_call(sums_kernel, out_shape=(jax.ShapeDtypeStruct((ROWS, SCANS)...  90.1 us
    pallas_call x1, Pallas kernels, band_call(): pl.pallas_call(band_kernel, out_shape=jax.ShapeDtypeStruct((BAND, SCANS,...  34.6 us
    pallas_call x1, Pallas kernels, update_call(): pl.pallas_call(update_kernel, out_shape=(jax.ShapeDtypeStruct((SLOTS, TIL...  14.5 us
    pallas_call x1, Pallas kernels, local(): pl.pallas_call(total_kernel, out_shape=jax.ShapeDtypeStruct((2,), F32), i...  14 us
    pallas_call x1, Pallas kernels, partials_call(): pl.pallas_call(partial_kernel, out_shape=(jax.ShapeDtypeStruct((BAND, TIL...  13.7 us

profile of v3, /device:TPU:1, one launch (start us, length us, event | category | flops | bytes accessed | tf_op | source)
XLA Modules:
  0.0 169.5 jit_solution(16072658619971337938)
XLA Ops:
  1.3 34.6 %band.1.band_h = bf16[14,384,512]{2,1,0:T(8,128)(2,1)} custom-call(bf16[384,3584]{1,0:T(8,128)(2,1)} %series_h.3), custom_call_target="tpu_custom_call" | custom-call | tf_op jit(solution)/shard_map/band/pallas_call | solution.py:704
  35.9 13.7 %partials.1 = (bf16[14,512,384]{2,1,0:T(8,128)(2,1)}, bf16[7,384,512]{2,1,0:T(8,128)(2,1)}) custom-call(s32[10]{0:T(128)} %bitcast.17, s32[10]{0:T(128)} %bitcast.19, s32[1]{0:T(128)} %bitcast.9.count_s, f32[10,512,512]{2,1,0:T(8,128)} %bitcast.11, bf16[384,3584]{1,0:T(8,128)(2,1)} %series_h.3, bf16[14,384,512]{2,1,0:T(8,128)(2,1)} %band.1.band_h), custom_call_target="tpu_custom_call" | custom-call | tf_op jit(solution)/shard_map/partials/pallas_call | solution.py:733
  49.7 90.1 %sums.1 = (bf16[7168,384]{1,0:T(8,128)(2,1)}, bf16[2688,512]{1,0:T(8,128)(2,1)}, f32[8,384]{1,0:T(8,128)}) custom-call(bf16[7168,384]{1,0:T(8,128)(2,1)} %bitcast.14, bf16[2688,512]{1,0:T(8,128)(2,1)} %bitcast.16), custom_call_target="tpu_custom_call" | custom-call | tf_op jit(solution)/shard_map/sums/pallas_call | solution.py:716
  139.8 14.5 %update.1 = (f32[10,512,512]{2,1,0:T(8,128)}, f32[8,128]{1,0:T(8,128)}) custom-call(s32[10]{0:T(128)} %bitcast.18, s32[10]{0:T(128)} %bitcast.20, s32[1]{0:T(128)} %bitcast.10.count_s, f32[10,512,512]{2,1,0:T(8,128)} %bitcast.12, bf16[14,512,384]{2,1,0:T(8,128)(2,1)} %bitcast.13, bf16[14,384,512]{2,1,0:T(8,128)(2,1)} %band.1.band_h, ...), custom_call_target="tpu_custom_call" | custom-call | tf_op jit(solution)/shard_map/update/pallas_call | solution.py:750
  154.3 14.0 %total.1 = f32[2]{0:T(128)} custom-call(f32[8,128]{1,0:T(8,128)} %get-tuple-element.14.sums, f32[8,384]{1,0:T(8,128)} %get-tuple-element.15.squares), custom_call_target="tpu_custom_call" | custom-call | tf_op jit(solution)/shard_map/total/pallas_call | solution.py:776
  168.4 1.1 copy.9

commit v4 on v3

--- a/solution.py
+++ b/solution.py
@@ -240,7 +240,7 @@
     dist = [(place.x - xs + 4) % 4, (xs - place.x + 4) % 4]
     onward = [place.at(x=(place.x + 1) % 4), place.at(x=(place.x + 3) % 4)]
     hops = [jnp.where(near, dist[s % 2], (dist[s % 2] + 4 - s // 2) % 4) for s in range(4)]
-    lag = [jnp.where(near, 0, s // 2 + 1) + hops[s] for s in range(4)]
+    lag = [jnp.where(near, 0, s // 2 + 1) + hops[s] + 1 - s // 2 for s in range(4)]
     crossing = [jnp.logical_and(near, dist[s % 2] == s // 2) for s in range(4)]
 
     def slot(i, which):
@@ -287,12 +287,21 @@
     @pl.when(source)
     def _():
         def emit(k, carry):
-            for s in range(4):
-                i = k * 4 + s
-                forward(native(i, series), i, s)
+            for s in (2, 3):
+                forward(native(k * 4 + s, series), k * 4 + s, s)
+
+            @pl.when(k > 0)
+            def _():
+                for s in (0, 1):
+                    i = (k - 1) * 4 + s
+                    forward(native(i, series), i, s)
+
             return carry
 
         lax.fori_loop(0, CHUNKS // 4, emit, 0)
+        for s in (0, 1):
+            i = CHUNKS - 4 + s
+            forward(native(i, series), i, s)
         load.wait()
 
         def hold(i, carry):
@@ -304,7 +313,7 @@
     @pl.when(jnp.logical_not(source))
     def _():
         def tick(t, carry):
-            for s in range(4):
+            for s in (2, 3, 0, 1):
                 k = t - lag[s]
 
                 @pl.when(jnp.logical_and(k >= 0, k < CHUNKS // 4))

time: 172 us -> 171 us (level); the launches traced: 169 us -> 171 us
  no operation moved by 1% of the time
where the time goes in v4:
time: 171 us
  Pallas kernels  168 us (98%)
    pallas_call x1, Pallas kernels, sums_call(): pl.pallas_call(sums_kernel, out_shape=(jax.ShapeDtypeStruct((ROWS, SCANS)...  88.5 us
    pallas_call x1, Pallas kernels, band_call(): pl.pallas_call(band_kernel, out_shape=jax.ShapeDtypeStruct((BAND, SCANS,...  34.7 us
    pallas_call x1, Pallas kernels, update_call(): pl.pallas_call(update_kernel, out_shape=(jax.ShapeDtypeStruct((SLOTS, TIL...  15.8 us
    pallas_call x1, Pallas kernels, partials_call(): pl.pallas_call(partial_kernel, out_shape=(jax.ShapeDtypeStruct((BAND, TIL...  14.7 us
    pallas_call x1, Pallas kernels, local(): pl.pallas_call(total_kernel, out_shape=jax.ShapeDtypeStruct((2,), F32), i...  14.5 us

profile of v4, /device:TPU:1, one launch (start us, length us, event | category | flops | bytes accessed | tf_op | source)
XLA Modules:
  0.0 170.6 jit_solution(5317975753098628448)
XLA Ops:
  1.3 34.7 %band.1.band_h = bf16[14,384,512]{2,1,0:T(8,128)(2,1)} custom-call(bf16[384,3584]{1,0:T(8,128)(2,1)} %series_h.3), custom_call_target="tpu_custom_call" | custom-call | tf_op jit(solution)/shard_map/band/pallas_call | solution.py:713
  35.9 14.7 %partials.1 = (bf16[14,512,384]{2,1,0:T(8,128)(2,1)}, bf16[7,384,512]{2,1,0:T(8,128)(2,1)}) custom-call(s32[10]{0:T(128)} %bitcast.17, s32[10]{0:T(128)} %bitcast.19, s32[1]{0:T(128)} %bitcast.9.count_s, f32[10,512,512]{2,1,0:T(8,128)} %bitcast.11, bf16[384,3584]{1,0:T(8,128)(2,1)} %series_h.3, bf16[14,384,512]{2,1,0:T(8,128)(2,1)} %band.1.band_h), custom_call_target="tpu_custom_call" | custom-call | tf_op jit(solution)/shard_map/partials/pallas_call | solution.py:742
  50.7 88.5 %sums.1 = (bf16[7168,384]{1,0:T(8,128)(2,1)}, bf16[2688,512]{1,0:T(8,128)(2,1)}, f32[8,384]{1,0:T(8,128)}) custom-call(bf16[7168,384]{1,0:T(8,128)(2,1)} %bitcast.14, bf16[2688,512]{1,0:T(8,128)(2,1)} %bitcast.16), custom_call_target="tpu_custom_call" | custom-call | tf_op jit(solution)/shard_map/sums/pallas_call | solution.py:725
  139.2 15.8 %update.1 = (f32[10,512,512]{2,1,0:T(8,128)}, f32[8,128]{1,0:T(8,128)}) custom-call(s32[10]{0:T(128)} %bitcast.18, s32[10]{0:T(128)} %bitcast.20, s32[1]{0:T(128)} %bitcast.10.count_s, f32[10,512,512]{2,1,0:T(8,128)} %bitcast.12, bf16[14,512,384]{2,1,0:T(8,128)(2,1)} %bitcast.13, bf16[14,384,512]{2,1,0:T(8,128)(2,1)} %band.1.band_h, ...), custom_call_target="tpu_custom_call" | custom-call | tf_op jit(solution)/shard_map/update/pallas_call | solution.py:759
  155.1 14.5 %total.1 = f32[2]{0:T(128)} custom-call(f32[8,128]{1,0:T(8,128)} %get-tuple-element.14.sums, f32[8,384]{1,0:T(8,128)} %get-tuple-element.15.squares), custom_call_target="tpu_custom_call" | custom-call | tf_op jit(solution)/shard_map/total/pallas_call | solution.py:785
  169.5 1.1 copy.9
